TPU v7x, 128 devices: a whole 4x4x4 slice. The times are simulated.
128 devices in a mesh: grid: 16 (over z_lo, y, core), pts: 8 (over x, z_hi).
Axes of the slice: x: 4, y: 4, z: 4 (z_hi: 2, z_lo: 2; z = z_hi * 2 + z_lo), core: 2. Of those that a mesh axis runs over, the one named last changes fastest.
Arguments:
- orbitals: bfloat16 [32768, 512], P(('grid', 'pts')), may hold values from -6 to 6
- point_rows: int32 [128, 8, 24], P(('grid', 'pts')), may hold values from 0 to 255, as said below
- point_count: int32 [128, 8], P(('grid', 'pts')), may hold values from 12 to 24, as said below
- potential: bfloat16 [24576, 8, 3072], P('pts', None, 'grid'), may hold values from -0.0016860962 to 0.0016860962
- fitted_basis: bfloat16 [32768, 24576], P('grid', 'pts'), may hold values from -0.0390625 to 0.0390625
Outputs:
- updated: bfloat16 [32768, 512], P(('grid', 'pts'))
- projection: bfloat16 [24576, 512], P('pts')
Inputs may be any that keep to these rules, and one draw needn't show every extreme that they name: `point_count`: each source device has at least one owner with all 24 slots valid. `point_rows`: the listed rows of one source device are all different.
All inputs are finite; a program needn't handle non-finite values.
Results may differ from a plain program's by a relative error of at most 0.0055.
Values may be sent and summed in bfloat16 or wider, within the bound.
No kernel may reach another device: no remote copies, remote signals or barrier semaphores. Data moves between devices by JAX's collectives and lax.ppermute only.
A program may use at most 128 MiB of HBM per device.

v0:
```python
import jax
import jax.numpy as jnp
from jax import lax
from jax.sharding import PartitionSpec as P


def on_device(orbitals, point_rows, point_count, potential, fitted_basis):
    width = orbitals.shape[1]
    owners = point_rows.shape[1]
    per_owner = point_rows.shape[2]
    picked = jnp.take(orbitals, point_rows[0], axis=0)
    valid_slot = lax.broadcasted_iota(jnp.int32, (owners, per_owner), 1) < point_count[0][:, None]
    picked = jnp.where(valid_slot[:, :, None], picked, jnp.zeros_like(picked))
    arrived = lax.all_to_all(picked, "pts", split_axis=0, concat_axis=0, tiled=True)
    slot_rows = arrived.reshape(owners * per_owner, width)
    own_points = lax.all_gather(slot_rows, "grid", axis=0, tiled=True)
    own_count = own_points.shape[0]
    pot_cols = potential.reshape(own_count, -1)
    piece = lax.all_gather(slot_rows, "pts", axis=0, tiled=True)
    pair_dens = jnp.dot(own_points, piece.T, preferred_element_type=jnp.float32)
    weighted = (pot_cols.astype(jnp.float32) * pair_dens).astype(jnp.bfloat16)
    proj_part = jnp.dot(weighted, piece, preferred_element_type=jnp.float32)
    projection = lax.psum(proj_part, "grid").astype(jnp.bfloat16)
    exchange = lax.psum_scatter(
        jnp.dot(fitted_basis, projection, preferred_element_type=jnp.float32),
        "pts",
        scatter_dimension=0,
        tiled=True,
    )
    updated = (orbitals.astype(jnp.float32) - exchange).astype(jnp.bfloat16)
    return (updated, projection)


def solution(mesh):
    in_specs = (
        P(("grid", "pts"), None),
        P(("grid", "pts"), None, None),
        P(("grid", "pts"), None),
        P("pts", None, "grid"),
        P("grid", "pts"),
    )
    out_specs = (P(("grid", "pts"), None), P("pts", None))
    return jax.shard_map(
        on_device, mesh=mesh, in_specs=in_specs, out_specs=out_specs, check_vma=False
    )
```

profile of v0, /device:TPU:0, one launch (start us, length us, event | category | flops | bytes accessed | tf_op | source)
XLA Modules:
  0.0 319.9 jit_solution(1531652905952017323)
XLA Ops:
  7.2 0.0 all-gather.5.cloned.1.call-start
  7.2 0.7 compare_select_fusion
  7.9 0.8 iota_compare_fusion
  8.7 0.1 reshape.70
  8.8 2.0 gather_fusion
  10.8 0.1 select_select_fusion
  10.9 15.8 %all_to_all.5 = bf16[8,24,512]{2,1,0:T(8,128)(2,1)} all-to-all(bf16[8,24,512]{2,1,0:T(8,128)(2,1)S(1)} %select_select_fusion), channel_id=1, replica_groups=mesh['grid'=16,'pts'=8] {'pts'}, dimensions={0} | all-to-all | bytes 393216 | tf_op jit(solution)/shard_map/all_to_all | solution.py:14
  26.7 0.0 all-gather.5.cloned.1.call-update
  26.8 0.0 all-gather.3.cloned.1.call-start
  26.8 0.7 all-gather.3.cloned.1.call-update
  27.5 0.0 reduce-scatter.2.cloned.1.call-start
  27.6 48.2 %all-gather.5.cloned.1.call-done = bf16[1536,512]{1,0:T(8,128)(2,1)} async-done(((bf16[192,512]{1,0:T(8,128)(2,1)}), bf16[1536,512]{1,0:T(8,128)(2,1)}) %all-gather.5.cloned.1.call-update) | async-done | bytes 1572880 | tf_op jit(solution)/shard_map/all_gather | solution.py:19
  75.7 35.6 %all-gather.3.cloned.1.call-done = bf16[3072,512]{1,0:T(8,128)(2,1)} async-done(((bf16[192,512]{1,0:T(8,128)(2,1)}), bf16[3072,512]{1,0:T(8,128)(2,1)}) %all-gather.3.cloned.1.call-update) | async-done | bytes 3145744 | tf_op jit(solution)/shard_map/all_gather | solution.py:16
  111.3 17.6 %fusion.1 = f32[3072,512]{1,0:T(8,128)} fusion(bf16[1536,512]{1,0:T(8,128)(2,1)} %all-gather.5.cloned.1.call-done, bf16[3072,1536]{0,1:T(8,128)(2,1)} %bitcast.24, bf16[3072,512]{1,0:T(8,128)(2,1)} %all-gather.3.cloned.1.call-done), kind=kOutput, calls=%fused_computation.4 | convolution fusion | flops 9677832192 | bytes 20447232 | tf_op jit(solution)/shard_map/dot_general | solution.py:22
  128.9 85.0 %all-reduce.1 = bf16[3072,512]{1,0:T(8,128)(2,1)S(1)} all-reduce(f32[3072,512]{1,0:T(8,128)} %fusion.1), channel_id=1, replica_groups=mesh['grid'=16,'pts'=8] {'grid'}, use_global_device_ids=true, to_apply=%region_0.1 | all-reduce | flops 1572864 | bytes 9437184 | tf_op jit(solution)/shard_map/psum | solution.py:23
  213.9 0.0 copy-start.1
  213.9 12.3 %convolution_bitcast_fusion = f32[2048,512]{0,1:T(8,128)} fusion(bf16[3072,512]{1,0:T(8,128)(2,1)S(1)} %all-reduce.1, bf16[2048,3072]{1,0:T(8,128)(2,1)} %param.9), kind=kOutput, calls=%fused_computation.3 | convolution fusion | flops 6442450944 | bytes 19922944 | tf_op jit(solution)/shard_map/dot_general | solution.py:25
  226.2 0.0 copy-done.1
  226.2 0.0 copy-start
  226.2 0.0 reduce-scatter.2.cloned.1.call-update
  226.2 0.9 copy-done
  227.1 0.1 copy.7
  227.3 84.1 %reduce-scatter.2.cloned.1.call-done = f32[256,512]{0,1:T(8,128)} async-done(((f32[2048,512]{0,1:T(8,128)}), f32[256,512]{0,1:T(8,128)}) %reduce-scatter.2.cloned.1.call-update) | async-done | bytes 524304 | tf_op jit(solution)/shard_map/reduce_scatter | solution.py:24
  311.4 1.1 subtract_convert_fusion
  312.5 0.8 copy.8
  (1 shorter events, 0.0 us)
Async XLA Ops:
  7.2 68.6 %all-gather.5.cloned.1.call-start = ((), (), s32[]{:S(2)}) async-start(), calls=%async_computation.3 | async-start | bytes 1769472 | tf_op jit(solution)/shard_map/all_gather | solution.py:19
  26.8 84.6 %all-gather.3.cloned.1.call-start = ((), (), s32[]{:S(2)}) async-start(), calls=%async_computation.2 | async-start | bytes 3342336 | tf_op jit(solution)/shard_map/all_gather | solution.py:16
  27.5 283.9 %reduce-scatter.2.cloned.1.call-start = ((), (), s32[]{:S(2)}) async-start(), calls=%async_computation.4 | async-start | bytes 4718592 | tf_op jit(solution)/shard_map/reduce_scatter | solution.py:24
  213.9 12.3 %copy-start.1 = (bf16[3072,512]{1,0:T(8,128)(2,1)}, bf16[3072,512]{1,0:T(8,128)(2,1)S(1)}, u32[]{:S(2)}) copy-start(bf16[3072,512]{1,0:T(8,128)(2,1)S(1)} %all-reduce.1) | copy-start | bytes 9437188
  226.2 1.0 copy-start
Sparse Core Ops, SparseCore 0:
  26.9 48.8 all-gather.4
  77.4 33.8 all-gather.2
  226.3 85.0 reduce-scatter.1
where the time goes:
time: 320 us
  waiting for transfers between devices  169 us (53%)
  blocking collectives  101 us (32%)
  matrix products  29.9 us (9%)
  between operations  13.8 us (4%)
  local copies, waits for them, and re-layouts  4.02 us (1%)
    psum x1, blocking collectives, on_device(): projection = lax.psum(proj_part, 'grid').astype(jnp.bfloat16)  85 us
    reduce_scatter x1, waiting for transfers between devices, on_device(): lax.psum_scatter(jnp.dot(fitted_basis, projection, preferred_element_type...  84.1 us
    all_gather x1, waiting for transfers between devices, on_device(): piece = lax.all_gather(slot_rows, 'pts', axis=0, tiled=True)  48.2 us
    all_gather x1, waiting for transfers between devices, on_device(): own_points = lax.all_gather(slot_rows, 'grid', axis=0, tiled=True)  35.6 us
    dot_general x1, matrix products, on_device(): proj_part = jnp.dot(weighted, piece, preferred_element_type=jnp.float32)  17.6 us
    all_to_all x1, blocking collectives, on_device(): lax.all_to_all(picked, 'pts', split_axis=0, concat_axis=0, tiled=True)  15.8 us
    dot_general x1, matrix products, on_device(): jnp.dot(fitted_basis, projection, preferred_element_type=jnp.float32)  12.3 us
  transfers between devices with their start and end apart: 3, of which 3 were waited for; matrix products, arithmetic and copies ran while one was open for 0% of the time, Pallas kernels for 0%

commit v1 on v0

v1 whole, which is shorter than its diff:
```python
import functools

import jax
import jax.numpy as jnp
from jax import lax
from jax.experimental import pallas as pl
from jax.experimental.pallas import tpu as pltpu
from jax.sharding import PartitionSpec as P


BF = jnp.bfloat16
F32 = jnp.float32
B = 512
SUB = 192
CH = 384
COLS = 1536
NY = 4
NX = 4
RT = 512
HB = 256


def grid_perm(zl=0, y=0, c=0):
    pairs = []
    for i in range(16):
        a, r = divmod(i, 8)
        b, d = divmod(r, 2)
        pairs.append((i, (((a + zl) % 2) * 4 + (b + y) % 4) * 2 + (d + c) % 2))
    return pairs


def pts_perm(x=0, zh=0):
    pairs = []
    for i in range(8):
        a, b = divmod(i, 2)
        pairs.append((i, ((a + x) % 4) * 2 + (b + zh) % 2))
    return pairs


def gmove(v, **shift):
    return lax.ppermute(v, "grid", grid_perm(**shift))


def pmove(v, **shift):
    return lax.ppermute(v, "pts", pts_perm(**shift))


def pick_body(rows_ref, count_ref, orb_ref, out_ref):
    lane = lax.broadcasted_iota(jnp.int32, (1, 24), 1)
    row = lax.broadcasted_iota(jnp.int32, (256, 24), 0)
    parts = []
    for q in range(8):
        index = jnp.where(lane < count_ref[0, q], rows_ref[0, q : q + 1, :], -1)
        parts.append((row == index).astype(BF))
    pick = jnp.concatenate(parts, axis=1)
    out_ref[...] = lax.dot_general(
        pick, orb_ref[...], (((0,), (0,)), ((), ())), preferred_element_type=F32
    ).astype(BF)


def pick_call(rows, count, orbitals):
    vm = pl.BlockSpec(memory_space=pltpu.VMEM)
    return pl.pallas_call(
        pick_body,
        out_shape=jax.ShapeDtypeStruct((SUB, B), BF),
        in_specs=[vm, pl.BlockSpec(memory_space=pltpu.SMEM), vm],
        out_specs=vm,
        name="pick",
    )(rows, count, orbitals)


def pair_body(n, kind, picks, meta_ref, piece_ref, pot_ref, *refs):
    count = 1 + max(i for block in picks for i, _ in block)
    arrays, rest = refs[:count], refs[count:]
    buf, sems = rest[-2:]
    core, same = meta_ref[0], meta_ref[1]

    def fetch(j):
        start = pl.multiple_of(meta_ref[2 + j] * CH, 128)
        return pltpu.make_async_copy(pot_ref.at[:, pl.ds(start, CH)], buf.at[j], sems.at[j])

    for j in range(n):
        fetch(j).start()
    is0 = core == 0
    pick_own = (same == 0) if kind == "send" else (same == 1)
    for j in range(n):
        near_m, far_m, near_o, far_o = [
            arrays[i][...] if at is None else arrays[i][at] for i, at in picks[j]
        ]
        m = jnp.where(pick_own, near_m, far_m)
        o = jnp.where(pick_own, near_o, far_o)
        rows = jnp.concatenate([jnp.where(is0, m, o), jnp.where(is0, o, m)], axis=0)
        dens = lax.dot_general(
            piece_ref[...], rows, (((1,), (1,)), ((), ())), preferred_element_type=F32
        )
        fetch(j).wait()
        w = (buf[j].astype(F32) * dens).astype(BF)
        out = lax.dot_general(
            w, piece_ref[...], (((0,), (0,)), ((), ())), preferred_element_type=F32
        )
        if kind == "send":
            rest[0][j] = out.astype(BF)
        elif kind == "keep":
            rest[0][...] = out
        elif kind == "first":
            got, top, low = rest[:3]
            out = (out + got[0].astype(F32)).astype(BF)
            top[...] = out[:SUB]
            low[...] = out[SUB:]
        else:
            got, near, o_ref = rest[0], rest[1 + j], rest[3 + j]
            out = out + got[j].astype(F32)
            add = near[...].astype(F32)
            top, low = (out[:SUB] + add, out[SUB:]) if j == 0 else (out[:SUB], out[SUB:] + add)
            o_ref[:SUB, :] = top.astype(BF)
            o_ref[SUB:, :] = low.astype(BF)


def pair_call(kind, meta, piece, pot_t, arrays, picks, extra=()):
    n = len(picks)
    vm = pl.BlockSpec(memory_space=pltpu.VMEM)
    shape = jax.ShapeDtypeStruct
    outs = {
        "send": [shape((n, CH, B), BF)],
        "keep": [shape((CH, B), F32)],
        "first": [shape((SUB, B), BF)] * 2,
        "second": [shape((CH, B), BF)] * 2,
    }[kind]
    return pl.pallas_call(
        functools.partial(pair_body, n, kind, picks),
        out_shape=outs,
        in_specs=[
            pl.BlockSpec(memory_space=pltpu.SMEM), vm, pl.BlockSpec(memory_space=pltpu.HBM)
        ] + [vm] * (len(arrays) + len(extra)),
        out_specs=[vm] * len(outs),
        scratch_shapes=[pltpu.VMEM((n, COLS, CH), BF), pltpu.SemaphoreType.DMA((n,))],
        compiler_params=pltpu.CompilerParams(vmem_limit_bytes=9 << 20),
        cost_estimate=pl.CostEstimate(
            flops=2 * n * CH * COLS * B * 2,
            bytes_accessed=n * COLS * CH * 2,
            transcendentals=0,
        ),
    )(meta, piece, pot_t, *arrays, *extra)


def exch_body(n, kind, places, meta_ref, fb_ref, *refs):
    ts, rest = refs[:n], refs[n:]
    k = sum(r.shape[0] for r in ts) // CH
    if kind == "first":
        out_ref, proj_ref, buf, sems, proj_sems, part, out_sems = rest
    elif kind == "next":
        acc_ref, _, out_ref, proj_ref, buf, sems, proj_sems, part, out_sems, acc, acc_sems = rest
    else:
        acc_ref, _, *x_sends, x_own, z_send, z_own, proj_ref, buf, sems, proj_sems, acc, acc_sems = rest

    def fetch(i, j):
        row = pl.multiple_of(meta_ref[1 + i] * RT, RT)
        start = pl.multiple_of(meta_ref[5 + j] * CH, 128)
        return pltpu.make_async_copy(
            fb_ref.at[pl.ds(row, RT), pl.ds(start, CH)],
            buf.at[i, :, pl.ds(j * CH, CH)],
            sems.at[i, j],
        )

    def before(i):
        row = pl.multiple_of(meta_ref[1 + i] * RT, RT)
        return pltpu.make_async_copy(acc_ref.at[pl.ds(row, RT)], acc.at[i], acc_sems.at[i])

    def store(i):
        return pltpu.make_async_copy(part.at[i], out_ref.at[pl.ds(i * RT, RT)], out_sems.at[i])

    def place(j):
        block, at = places[j]
        row = pl.multiple_of(meta_ref[5 + block] * CH + at, SUB)
        return pltpu.make_async_copy(
            ts[j], proj_ref.at[pl.ds(row, ts[j].shape[0])], proj_sems.at[j]
        )

    def begin(i):
        for j in range(k):
            fetch(i, j).start()
        if kind != "first":
            before(i).start()

    begin(0)
    begin(1)
    t = jnp.concatenate([r[...] for r in ts], axis=0)
    zh = meta_ref[0]
    for i in range(4):
        for j in range(k):
            fetch(i, j).wait()
        if i < 2:
            begin(i + 2)
        if i == 1:
            for j in range(n):
                place(j).start()
        d = jnp.dot(buf[i], t, preferred_element_type=F32)
        if kind != "first":
            before(i).wait()
            d = d + acc[i]
        if kind != "last":
            part[i] = d
            store(i).start()
            continue
        if i < 3:
            x_sends[i][...] = d[:, :HB].astype(BF)
        else:
            x_own[...] = d[:, :HB]
        lo, hi = d[:256, HB:], d[256:, HB:]
        z_send[i] = jnp.where(zh == 0, hi, lo).astype(BF)
        z_own[i] = jnp.where(zh == 0, lo, hi)
    if kind != "last":
        for i in range(4):
            store(i).wait()
    for j in range(n):
        place(j).wait()


def exch_call(kind, zh, order, cols, fb, ts, acc=None, proj=None):
    n, k = len(ts), len(cols)
    vm = pl.BlockSpec(memory_space=pltpu.VMEM)
    hbm = pl.BlockSpec(memory_space=pltpu.HBM)
    shape = jax.ShapeDtypeStruct
    tile = pltpu.VMEM((4, RT, B), F32)
    dma = pltpu.SemaphoreType.DMA
    scratch = [pltpu.VMEM((4, RT, k * CH), BF), dma((4, k)), dma((n,))]
    if kind != "last":
        scratch += [tile, dma((4,))]
    if kind != "first":
        scratch += [tile, dma((4,))]
    outs, out_specs = [pltpu.HBM((4 * RT, B), F32)], [hbm]
    if kind == "last":
        outs = [shape((RT, HB), BF)] * 3 + [
            shape((RT, HB), F32), shape((4, 256, HB), BF), shape((4, 256, HB), F32)
        ]
        out_specs = [vm] * len(outs)
    outs, out_specs = outs + [pltpu.HBM((8 * CH, B), BF)], out_specs + [hbm]
    places, row = [], 0
    for t in ts:
        places.append((row // CH, row % CH))
        row += t.shape[0]
    args = [] if acc is None else [acc, proj]
    args = [pltpu.with_memory_space_constraint(v, pltpu.HBM) for v in args]
    return pl.pallas_call(
        functools.partial(exch_body, n, kind, places),
        out_shape=outs,
        in_specs=[pl.BlockSpec(memory_space=pltpu.SMEM), hbm] + [vm] * n + [hbm] * len(args),
        out_specs=out_specs,
        input_output_aliases={} if acc is None else {3 + n: len(outs) - 1},
        scratch_shapes=scratch,
        compiler_params=pltpu.CompilerParams(
            vmem_limit_bytes={"first": 11, "next": 21, "last": 13}[kind] << 20
        ),
        cost_estimate=pl.CostEstimate(
            flops=2 * 4 * RT * CH * k * B,
            bytes_accessed=4 * RT * CH * k * 2,
            transcendentals=0,
        ),
    )(jnp.stack([zh] + order + cols).astype(jnp.int32), fb, *ts, *args)


def small_call(body, outs, *args, smem=0, aliases=None):
    vm = pl.BlockSpec(memory_space=pltpu.VMEM)
    return pl.pallas_call(
        body,
        out_shape=outs,
        in_specs=[pl.BlockSpec(memory_space=pltpu.SMEM)] * smem + [vm] * (len(args) - smem),
        out_specs=[vm] * len(outs),
        input_output_aliases=aliases or {},
        compiler_params=pltpu.CompilerParams(vmem_limit_bytes=6 << 20),
    )(*args)


def piece_body(blocks, at_ref, *refs):
    out_ref = refs[-1]
    for i in range(blocks):
        for q in range(8):
            out_ref[q, at_ref[2 * i], at_ref[2 * i + 1]] = refs[i][q]


def cut_body(rows_a, rows_b, a_ref, b_ref, a_out, b_out):
    a_out[...] = a_ref[rows_a]
    b_out[...] = b_ref[rows_b]


def zsum_body(own_ref, got_ref, *outs):
    for i in range(4):
        outs[i][...] = (own_ref[i] + got_ref[i].astype(F32)).astype(outs[i].dtype)


def step(orbitals, point_rows, point_count, potential, fitted_basis):
    g, p = lax.axis_index("grid"), lax.axis_index("pts")
    zl, y, c = g // 8, (g // 2) % NY, g % 2
    x, zh = p // 2, p % 2
    i32 = jnp.int32
    fitted_basis = pltpu.with_memory_space_constraint(fitted_basis, pltpu.HBM)

    picked = pick_call(point_rows, point_count, orbitals)
    xa0 = pmove(picked, x=1)
    xb0 = pmove(picked, x=-1)
    zpart = pmove(picked, zh=1)
    xa1 = pmove(zpart, x=1)
    xb1 = pmove(zpart, x=-1)
    x2a = pmove(xa0, x=1)
    x2b = pmove(xb1, x=-1)
    spots = []
    for v, s, at in (
        (picked, 0, zh), (zpart, 0, 1 - zh), (xa0, -1, zh), (xa1, -1, 1 - zh),
        (xb0, 1, zh), (xb1, 1, 1 - zh), (x2a, 2, zh), (x2b, 2, 1 - zh),
    ):
        spots.append((v.reshape(8, 24, B), (x + s) % NX, at))
    shape = jax.ShapeDtypeStruct((8, NX, 2, 24, B), BF)
    for name, some in (("k_piece1", spots[:6]), ("k_piece2", spots[6:])):
        at = jnp.stack([i for _, a, b in some for i in (a, b)]).astype(i32)
        args = [v for v, _, _ in some]
        if name == "k_piece2":
            args.append(piece)
        (piece,) = small_call(
            functools.partial(piece_body, len(some)), [shape], at, *args,
            smem=1, aliases={len(args): 0} if name == "k_piece2" else None,
        )
    piece = piece.reshape(COLS, B)

    slot = lax.all_to_all(picked.reshape(8, 24, B), "pts", 0, 0, tiled=True)
    slot = slot.reshape(SUB, B)
    rz = gmove(slot, zl=1)
    mine0 = jnp.stack([slot, rz])
    part0 = gmove(mine0, c=1)
    blk_a = gmove(mine0, y=1)
    blk_b = gmove(mine0, y=-1)
    part_a = gmove(blk_a, c=1)
    part_b = gmove(blk_b, c=1)
    rows = jax.ShapeDtypeStruct((SUB, B), BF)
    cut_a, cut_b = small_call(functools.partial(cut_body, 0, 1), [rows, rows], blk_a, blk_b)
    far_0 = gmove(cut_a, y=1)
    far_1 = gmove(cut_b, y=-1)
    part_0 = gmove(far_0, c=1)
    part_1 = gmove(far_1, c=1)

    pot_t = jnp.transpose(potential, (1, 2, 0)).reshape(COLS, 8 * CH)
    pot_t = pltpu.with_memory_space_constraint(pot_t, pltpu.HBM)
    same = (zl == c).astype(i32)

    def pairs(kind, shifts, arrays, picks, extra=()):
        core = 1 - c if kind == "send" else c
        meta = jnp.stack([c, same] + [core * NY + (y + s) % NY for s in shifts]).astype(i32)
        return pair_call(kind, meta, piece, pot_t, arrays, picks, extra)

    rows0 = [mine0, part0], [[(0, 0), (0, 1), (1, 0), (1, 1)]]
    rows1 = [blk_a, blk_b, part_a, part_b], [
        [(k, 0), (k, 1), (2 + k, 0), (2 + k, 1)] for k in range(2)
    ]
    rows2 = [far_0, far_1, part_0, part_1], [[(k, None) for k in range(4)]]
    (send0,) = pairs("send", [0], *rows0)
    got0 = gmove(send0, c=1)
    top, low = pairs("first", [0], *rows0, (got0,))
    ya = gmove(top, y=1)
    yb = gmove(low, y=-1)
    (send1,) = pairs("send", [-1, 1], *rows1)
    got1 = gmove(send1, c=1)
    to_a, to_b = pairs("second", [-1, 1], *rows1, (got1, ya, yb))
    ra = gmove(to_a, y=1)
    rb = gmove(to_b, y=-1)
    (send2,) = pairs("send", [2], *rows2)
    got2 = gmove(send2, c=1)
    (keep2,) = pairs("keep", [2], *rows2)
    total = keep2 + got2[0].astype(F32) + ra.astype(F32) + rb.astype(F32)
    total = total.astype(BF)
    zs = gmove(total, zl=1)

    t0 = (total.astype(F32) + zs.astype(F32)).astype(BF)
    ta = gmove(t0, y=1)
    tb = gmove(t0, y=-1)
    q0 = gmove(t0, c=1)
    cut_a, cut_b = small_call(
        functools.partial(cut_body, slice(0, SUB), slice(SUB, CH)), [rows, rows], ta, tb
    )
    t2a = gmove(cut_a, y=1)
    t2b = gmove(cut_b, y=-1)
    qa = gmove(ta, c=1)
    qb = gmove(tb, c=1)
    q2a = gmove(t2a, c=1)
    q2b = gmove(t2b, c=1)
    d = 1 - c
    col = lambda core, s: core * NY + (y + s) % NY
    ident = [jnp.int32(i) for i in range(4)]
    acc, proj = exch_call("first", zh, ident, [col(c, 2), col(d, 2)], fitted_basis, [t0, q0])
    cols = [col(c, 1), col(c, 3), col(d, 1), col(d, 3)]
    acc, proj = exch_call("next", zh, ident, cols, fitted_basis, [ta, tb, qa, qb], acc, proj)
    order = [(x + s) % NX for s in (2, 1, -1, 0)]
    x_2, x_1, x_3, x_own, z_send, z_own, projection = exch_call(
        "last", zh, order, [col(c, 0), col(d, 0)], fitted_basis,
        [t2a, t2b, q2a, q2b], acc, proj,
    )

    def over_x(to_2, to_1, to_3, own):
        total = own
        for v, s in ((to_2, 2), (to_1, 1), (to_3, -1)):
            total = total + pmove(v, x=s).astype(F32)
        return total

    z_got = pmove(z_send, zh=1)
    x_sum = over_x(x_2, x_1, x_3, x_own)
    quarter = lambda dtype: jax.ShapeDtypeStruct((256, HB), dtype)
    z_parts = small_call(zsum_body, [quarter(BF)] * 3 + [quarter(F32)], z_own, z_got)
    right = over_x(*z_parts)
    lo, hi = x_sum[:256], x_sum[256:]
    left = jnp.where(zh == 0, lo, hi) + pmove(
        jnp.where(zh == 0, hi, lo).astype(BF), zh=1
    ).astype(F32)
    exchange = jnp.concatenate([left, right], axis=1)
    updated = (orbitals.astype(F32) - exchange).astype(BF)
    return (updated, projection)


def solution(mesh):
    in_specs = (
        P(("grid", "pts"), None),
        P(("grid", "pts"), None, None),
        P(("grid", "pts"), None),
        P("pts", None, "grid"),
        P("grid", "pts"),
    )
    out_specs = (P(("grid", "pts"), None), P("pts", None))
    return jax.shard_map(step, mesh=mesh, in_specs=in_specs, out_specs=out_specs, check_vma=False)
```

time: 320 us -> 177 us (0.55)
  waiting for transfers between devices: 169 us -> 49.4 us
  blocking collectives: 101 us -> 15.9 us
  Pallas kernels: 0 us -> 50.1 us
  starting transfers between devices: 0.12 us -> 48.3 us
  matrix products: 29.9 us -> 0 us
  between operations: 13.8 us -> 0.92 us
  local copies, waits for them, and re-layouts: 4.02 us -> 8.01 us
    psum x1 -> x0, blocking collectives: 85 us -> none  [on_device(): projection = lax.psum(proj_part, 'grid').astype(jnp.bfloat16)]
    reduce_scatter x1 -> x0, waiting for transfers between devices: 84.1 us -> none  [on_device(): lax.psum_scatter(jnp.dot(fitted_basis, projection, preferred_element_type...]
    all_gather x2 -> x0, waiting for transfers between devices: 83.8 us -> none  [the longest x1 48.2 us: on_device(): piece = lax.all_gather(slot_rows, 'pts', axis=0, tiled=True)]
    pallas_call x0 -> x15, Pallas kernels: none -> 50.1 us  [the longest x6 24.7 us: pair_call(): pl.pallas_call(functools.partial(pair_body, n, kind, picks), out_shape=ou...]
    ppermute x0 -> x42, waiting for transfers between devices: none -> 49.4 us  [the longest x27 31.2 us: gmove(): return lax.ppermute(v, 'grid', grid_perm(**shift))]
    ppermute x0 -> x42, starting transfers between devices: none -> 48.3 us  [the longest x27 24.7 us: gmove(): return lax.ppermute(v, 'grid', grid_perm(**shift))]
    dot_general x2 -> x0, matrix products: 29.9 us -> none  [the longest x1 17.6 us: on_device(): proj_part = jnp.dot(weighted, piece, preferred_element_type=jnp.float32)]
    unnamed x6 -> x20, local copies, waits for them, and re-layouts: 1.91 us -> 7.09 us
  transfers between devices with their start and end apart: 3 -> 42, of which waited for: 3 -> 13; matrix products, arithmetic and copies ran while one was open for 0% -> 2% of each run, Pallas kernels for 0% -> 24%
where the time goes in v1:
time: 177 us; the launch traced here: 176 us
  Pallas kernels  50.1 us (28%)
  waiting for transfers between devices  49.4 us (28%)
  starting transfers between devices  48.3 us (27%)
  blocking collectives  15.9 us (9%)
  local copies, waits for them, and re-layouts  8.01 us (5%)
  other arithmetic  3.34 us (2%)
    ppermute x27, waiting for transfers between devices, gmove(): return lax.ppermute(v, 'grid', grid_perm(**shift))  31.2 us
    ppermute x27, starting transfers between devices, gmove(): return lax.ppermute(v, 'grid', grid_perm(**shift))  24.7 us
    pallas_call x6, Pallas kernels, pair_call(): pl.pallas_call(functools.partial(pair_body, n, kind, picks), out_shape=ou...  24.7 us
    ppermute x15, starting transfers between devices, pmove(): return lax.ppermute(v, 'pts', pts_perm(**shift))  23.6 us
    pallas_call x3, Pallas kernels, exch_call(): pl.pallas_call(functools.partial(exch_body, n, kind, places), out_shape=o...  20.4 us
    ppermute x15, waiting for transfers between devices, pmove(): return lax.ppermute(v, 'pts', pts_perm(**shift))  18.2 us
    all_to_all x1, blocking collectives, step(): slot = lax.all_to_all(picked.reshape(8, 24, B), 'pts', 0, 0, tiled=True)  15.9 us
    unnamed x20, local copies, waits for them, and re-layouts  7.09 us
  transfers between devices with their start and end apart: 42, of which 13 were waited for; matrix products, arithmetic and copies ran while one was open for 2% of the time, Pallas kernels for 24%

profile of v1, /device:TPU:0, one launch (start us, length us, event | category | flops | bytes accessed | tf_op | source)
XLA Modules:
  0.0 176.0 jit_solution(10883418263234669575)
XLA Ops:
  0.6 2.0 %pick.1 = bf16[192,512]{1,0:T(8,128)(2,1)} custom-call(s32[1,8,24]{2,1,0:T(8,128)} %rows_ref.1, s32[1,8]{1,0:T(1,128)} %count_ref.1, bf16[256,512]{1,0:T(8,128)(2,1)} %orb_ref.1), custom_call_target="tpu_custom_call" | custom-call | tf_op jit(solution)/shard_map/pick/pallas_call | solution.py:63
  2.7 15.9 %all_to_all.5 = bf16[8,24,512]{2,1,0:T(8,128)(2,1)S(1)} all-to-all(bf16[8,24,512]{2,1,0:T(8,128)(2,1)} %bitcast.42), channel_id=1, replica_groups=mesh['grid'=16,'pts'=8] {'pts'}, dimensions={0} | all-to-all | bytes 393216 | tf_op jit(solution)/shard_map/all_to_all | solution.py:324
  18.6 1.0 collective-permute-start.7
  19.6 4.7 %collective-permute-done.7 = bf16[192,512]{1,0:T(8,128)(2,1)S(1)} collective-permute-done((bf16[192,512]{1,0:T(8,128)(2,1)S(1)}, bf16[192,512]{1,0:T(8,128)(2,1)S(1)}, u32[]{:S(2)}, u32[]{:S(2)}) %collective-permute-start.7) | collective-permute-done | bytes 196640 | tf_op jit(solution)/shard_map/ppermute | solution.py:41
  24.3 1.6 collective-permute-start.8
  25.9 1.7 collective-permute-start.9
  27.6 1.1 collective-permute-start.2
  29.3 2.7 %collective-permute-start.6 = (bf16[192,512]{1,0:T(8,128)(2,1)}, bf16[192,512]{1,0:T(8,128)(2,1)S(1)}, u32[]{:S(2)}, u32[]{:S(2)}) collective-permute-start(bf16[192,512]{1,0:T(8,128)(2,1)} %pick.1), channel_id=1, source_target_pairs={{0,6},{1,7},{2,0},{3,1},{4,2},{5,3},{6,4},{7,5},{8,14},{9,15},{10,... | collective-permute-start | bytes 589832 | tf_op jit(solution)/shard_map/ppermute | solution.py:45
  32.0 3.0 %collective-permute-done.2 = bf16[192,512]{1,0:T(8,128)(2,1)S(1)} collective-permute-done((bf16[192,512]{1,0:T(8,128)(2,1)}, bf16[192,512]{1,0:T(8,128)(2,1)S(1)}, u32[]{:S(2)}, u32[]{:S(2)}) %collective-permute-start.2) | collective-permute-done | bytes 196640 | tf_op jit(solution)/shard_map/ppermute | solution.py:45
  35.0 1.1 collective-permute-start.3
  39.4 1.3 collective-permute-done.3
  40.7 2.2 %collective-permute-done.5 = bf16[192,512]{1,0:T(8,128)(2,1)S(1)} collective-permute-done((bf16[192,512]{1,0:T(8,128)(2,1)S(1)}, bf16[192,512]{1,0:T(8,128)(2,1)S(1)}, u32[]{:S(2)}, u32[]{:S(2)}) %collective-permute-start.5) | collective-permute-done | bytes 196640 | tf_op jit(solution)/shard_map/ppermute | solution.py:45
  45.2 0.9 copy-done
  49.5 1.1 shard_map.68.refs_2_
  51.4 1.1 shard_map.69
  52.4 5.7 %shard_map.73 = bf16[2,384,512]{2,1,0:T(8,128)(2,1)} custom-call(s32[4]{0:T(128)S(1)} %pad_add_fusion.6.meta_ref, bf16[1536,512]{1,0:T(8,128)(2,1)S(1)} %bitcast.36, bf16[1536,3072]{1,0:T(8,128)(2,1)} %bitcast.47, bf16[2,192,512]{2,1,0:T(8,128)(2,1)S(1)} %collective-permute-done.8.a_ref.refs_0_, ...), custom_call_target="tpu_custom_call" | custom-call | flops 2415919104 | bytes 2359296 | tf_op jit(solution)/shard_map/pallas_call | solution.py:129
  58.4 3.7 %shard_map.74 = bf16[1,384,512]{2,1,0:T(8,128)(2,1)} custom-call(s32[3]{0:T(128)S(1)} %get-tuple-element.50.meta_ref, bf16[1536,512]{1,0:T(8,128)(2,1)S(1)} %bitcast.37, bf16[1536,3072]{1,0:T(8,128)(2,1)} %bitcast.48, bf16[2,192,512]{2,1,0:T(8,128)(2,1)S(1)} %pad_maximum_fusion.refs_0_, bf16[2,192,512]{2,1,0:T(8,128)(2,1)S(1)} %collective-permute-done.18.refs_1_), custom_call_target="tpu_custom_call" | custom-call | flops 1207959552 | bytes 1179648 | tf_op jit(solution)/shard_map/pallas_call | solution.py:129
  64.1 2.4 %collective-permute-start.11 = (bf16[192,512]{1,0:T(8,128)(2,1)}, bf16[192,512]{1,0:T(8,128)(2,1)}, u32[]{:S(2)}, u32[]{:S(2)}) collective-permute-start(bf16[192,512]{1,0:T(8,128)(2,1)} %get-tuple-element.26), channel_id=1, source_target_pairs={{0,48},{8,56},{16,0},{24,8},{32,16},{40,24},{48,32},{56,40},{64,11... | collective-permute-start | bytes 589832 | tf_op jit(solution)/shard_map/ppermute | solution.py:41
  66.5 5.3 %collective-permute-done.10.refs_0_ = bf16[192,512]{1,0:T(8,128)(2,1)} collective-permute-done((bf16[192,512]{1,0:T(8,128)(2,1)}, bf16[192,512]{1,0:T(8,128)(2,1)}, u32[]{:S(2)}, u32[]{:S(2)}) %collective-permute-start.10) | collective-permute-done | bytes 196640 | tf_op jit(solution)/shard_map/ppermute | solution.py:41
  72.3 3.4 %shard_map.75 = (bf16[192,512]{1,0:T(8,128)(2,1)S(1)}, bf16[192,512]{1,0:T(8,128)(2,1)S(1)}) custom-call(s32[3]{0:T(128)S(1)} %get-tuple-element.51.meta_ref, bf16[1536,512]{1,0:T(8,128)(2,1)S(1)} %bitcast.38, bf16[1536,3072]{1,0:T(8,128)(2,1)} %bitcast.49, bf16[2,192,512]{2,1,0:T(8,128)(2,1)S(1)} %pad_maximum_fusion.refs_0_, ...), custom_call_target="tpu_custom_call" | custom-call | flops 1207959552 | bytes 1179648 | tf_op jit(solution)/shard_map/pallas_call | solution.py:129
  76.0 3.0 %collective-permute-start.21 = (bf16[192,512]{1,0:T(8,128)(2,1)S(1)}, bf16[192,512]{1,0:T(8,128)(2,1)S(1)}, u32[]{:S(2)}, u32[]{:S(2)}) collective-permute-start(bf16[192,512]{1,0:T(8,128)(2,1)S(1)} %get-tuple-element.28), channel_id=1, source_target_pairs={{0,48},{8,56},{16,0},{24,8},{32,16},{40,24},{48,32},{56,40},{64,11... | collective-permute-start | bytes 589832 | tf_op jit(solution)/shard_map/ppermute | solution.py:41
  79.1 3.4 %shard_map.72 = bf16[1,384,512]{2,1,0:T(8,128)(2,1)S(1)} custom-call(s32[3]{0:T(128)S(1)} %get-tuple-element.48.meta_ref, bf16[1536,512]{1,0:T(8,128)(2,1)S(1)} %bitcast.39, bf16[1536,3072]{1,0:T(8,128)(2,1)} %bitcast.50, bf16[192,512]{1,0:T(8,128)(2,1)} %collective-permute-done.10.refs_0_, bf16[192,512]{1,0:T(8,128)(2,1)} %collective-permute-done.11.refs_1_, ...), custom_call_target="tpu_custom_call" | custom-call | flops 1207959552 | bytes 1179648 | tf_op jit(solution)/shard_map/pallas_call | solution.py:129
  82.7 1.2 collective-permute-done.20.refs_5_
  83.8 5.1 %shard_map.76 = (bf16[384,512]{1,0:T(8,128)(2,1)S(1)}, bf16[384,512]{1,0:T(8,128)(2,1)S(1)}) custom-call(s32[4]{0:T(128)S(1)} %pad_add_fusion.4.meta_ref, bf16[1536,512]{1,0:T(8,128)(2,1)S(1)} %bitcast.40, bf16[1536,3072]{1,0:T(8,128)(2,1)} %bitcast.51, bf16[2,192,512]{2,1,0:T(8,128)(2,1)S(1)} %collective-permute-done.8.a_ref.refs_0_, ...), custom_call_target="tpu_custom_call" | custom-call | flops 2415919104 | bytes 2359296 | tf_op jit(solution)/shard_map/pallas_call | solution.py:129
  88.9 1.2 collective-permute-start.22
  90.1 2.1 %collective-permute-start.23 = (bf16[384,512]{1,0:T(8,128)(2,1)S(1)}, bf16[384,512]{1,0:T(8,128)(2,1)S(1)}, u32[]{:S(2)}, u32[]{:S(2)}) collective-permute-start(bf16[384,512]{1,0:T(8,128)(2,1)S(1)} %get-tuple-element.30), channel_id=1, source_target_pairs={{0,48},{8,56},{16,0},{24,8},{32,16},{40,24},{48,32},{56,40},{64,11... | collective-permute-start | bytes 1179656 | tf_op jit(solution)/shard_map/ppermute | solution.py:41
  92.2 3.4 %shard_map.71 = f32[384,512]{1,0:T(8,128)S(1)} custom-call(s32[3]{0:T(128)S(1)} %get-tuple-element.52.meta_ref, bf16[1536,512]{1,0:T(8,128)(2,1)S(1)} %bitcast.41, bf16[1536,3072]{1,0:T(8,128)(2,1)} %bitcast.52, bf16[192,512]{1,0:T(8,128)(2,1)} %collective-permute-done.10.refs_0_, bf16[192,512]{1,0:T(8,128)(2,1)} %collective-permute-done.11.refs_1_, ...), custom_call_target="tpu_custom_call" | custom-call | flops 1207959552 | bytes 1179648 | tf_op jit(solution)/shard_map/pallas_call | solution.py:129
  95.7 4.9 %collective-permute-done.22 = bf16[384,512]{1,0:T(8,128)(2,1)S(1)} collective-permute-done((bf16[384,512]{1,0:T(8,128)(2,1)S(1)}, bf16[384,512]{1,0:T(8,128)(2,1)S(1)}, u32[]{:S(2)}, u32[]{:S(2)}) %collective-permute-start.22) | collective-permute-done | bytes 393248 | tf_op jit(solution)/shard_map/ppermute | solution.py:41
  100.8 1.1 collective-permute-start.24
  101.9 8.5 %collective-permute-done.24 = bf16[384,512]{1,0:T(8,128)(2,1)S(1)} collective-permute-done((bf16[384,512]{1,0:T(8,128)(2,1)S(1)}, bf16[384,512]{1,0:T(8,128)(2,1)S(1)}, u32[]{:S(2)}, u32[]{:S(2)}) %collective-permute-start.24) | collective-permute-done | bytes 393248 | tf_op jit(solution)/shard_map/ppermute | solution.py:41
  110.5 1.2 collective-permute-start.25
  111.7 2.1 %collective-permute-start.26 = (bf16[384,512]{1,0:T(8,128)(2,1)S(1)}, bf16[384,512]{1,0:T(8,128)(2,1)S(1)}, u32[]{:S(2)}, u32[]{:S(2)}) collective-permute-start(bf16[384,512]{1,0:T(8,128)(2,1)S(1)} %add_convert_fusion.refs_0_), channel_id=1, source_target_pairs={{0,48},{8,56},{16,0},{24,8},{32,16},{40,24},{48,32},{56,40},{64,11... | collective-permute-start | bytes 1179656 | tf_op jit(solution)/shard_map/ppermute | solution.py:41
  113.8 6.6 %collective-permute-done.25.a_ref.refs_0_ = bf16[384,512]{1,0:T(8,128)(2,1)S(1)} collective-permute-done((bf16[384,512]{1,0:T(8,128)(2,1)S(1)}, bf16[384,512]{1,0:T(8,128)(2,1)S(1)}, u32[]{:S(2)}, u32[]{:S(2)}) %collective-permute-start.25) | collective-permute-done | bytes 393248 | tf_op jit(solution)/shard_map/ppermute | solution.py:41
  121.1 3.2 %collective-permute-start.28 = (bf16[192,512]{1,0:T(8,128)(2,1)S(1)}, bf16[192,512]{1,0:T(8,128)(2,1)S(1)}, u32[]{:S(2)}, u32[]{:S(2)}) collective-permute-start(bf16[192,512]{1,0:T(8,128)(2,1)S(1)} %get-tuple-element.32), channel_id=1, source_target_pairs={{0,48},{8,56},{16,0},{24,8},{32,16},{40,24},{48,32},{56,40},{64,11... | collective-permute-start | bytes 589832 | tf_op jit(solution)/shard_map/ppermute | solution.py:41
  124.5 5.7 %shard_map.78 = (f32[2048,512]{1,0:T(8,128)}, bf16[3072,512]{1,0:T(8,128)(2,1)}) custom-call(s32[7]{0:T(128)S(1)} %stack.160.meta_ref, bf16[2048,3072]{1,0:T(8,128)(2,1)} %fb_ref.5, bf16[384,512]{1,0:T(8,128)(2,1)S(1)} %add_convert_fusion.refs_0_, bf16[384,512]{1,0:T(8,128)(2,1)S(1)} %collective-permute-done.33.refs_1_), custom_call_target="tpu_custom_call" | custom-call | flops 1610612736 | bytes 3145728 | tf_op jit(solution)/shard_map/pallas_call | solution.py:244
  130.8 8.8 %shard_map.79 = (f32[2048,512]{1,0:T(8,128)}, bf16[3072,512]{1,0:T(8,128)(2,1)}) custom-call(s32[9]{0:T(128)S(1)} %stack.159.meta_ref, bf16[2048,3072]{1,0:T(8,128)(2,1)} %fb_ref.5, bf16[384,512]{1,0:T(8,128)(2,1)S(1)} %collective-permute-done.25.a_ref.refs_0_, ...), custom_call_target="tpu_custom_call", output_to_operand_aliasing={{1}: (7, {})} | custom-call | flops 3221225472 | bytes 6291456 | tf_op jit(solution)/shard_map/pallas_call | solution.py:244
  139.6 5.9 %shard_map.80 = (bf16[512,256]{1,0:T(8,128)(2,1)}, bf16[512,256]{1,0:T(8,128)(2,1)S(1)}, bf16[512,256]{1,0:T(8,128)(2,1)S(1)}, f32[512,256]{1,0:T(8,128)S(1)}, b...) custom-call(s32[7]{0:T(128)S(1)} %stack.136.meta_ref, ...), custom_call_target="tpu_custom_call", output_to_operand_aliasing={{6}: (7, {})} | custom-call | flops 1610612736 | bytes 3145728 | tf_op jit(solution)/shard_map/pallas_call | solution.py:244
  145.6 1.8 %collective-permute-start.34 = (bf16[512,256]{1,0:T(8,128)(2,1)}, bf16[512,256]{1,0:T(8,128)(2,1)S(1)}, u32[]{:S(2)}, u32[]{:S(2)}) collective-permute-start(bf16[512,256]{1,0:T(8,128)(2,1)} %get-tuple-element.38), channel_id=1, source_target_pairs={{0,4},{1,5},{2,6},{3,7},{4,0},{5,1},{6,2},{7,3},{8,12},{9,13},{10,... | collective-permute-start | bytes 786440 | tf_op jit(solution)/shard_map/ppermute | solution.py:45
  148.2 2.5 %collective-permute-start.36 = (bf16[512,256]{1,0:T(8,128)(2,1)S(1)}, bf16[512,256]{1,0:T(8,128)(2,1)}, u32[]{:S(2)}, u32[]{:S(2)}) collective-permute-start(bf16[512,256]{1,0:T(8,128)(2,1)S(1)} %get-tuple-element.40), channel_id=1, source_target_pairs={{0,6},{1,7},{2,0},{3,1},{4,2},{5,3},{6,4},{7,5},{8,14},{9,15},{10,... | collective-permute-start | bytes 786440 | tf_op jit(solution)/shard_map/ppermute | solution.py:45
  150.6 2.6 %collective-permute-start.38 = (bf16[4,256,256]{2,1,0:T(8,128)(2,1)S(1)}, bf16[4,256,256]{2,1,0:T(8,128)(2,1)S(1)}, u32[]{:S(2)}, u32[]{:S(2)}) collective-permute-start(bf16[4,256,256]{2,1,0:T(8,128)(2,1)S(1)} %get-tuple-element.42), channel_id=1, source_target_pairs={{0,1},{1,0},{2,3},{3,2},{4,5},{5,4},{6,7},{7,6},{8,9},{9,8},{10,11... | collective-permute-start | bytes 1572872 | tf_op jit(solution)/shard_map/ppermute | solution.py:45
  153.2 3.4 %collective-permute-done.34 = bf16[512,256]{1,0:T(8,128)(2,1)S(1)} collective-permute-done((bf16[512,256]{1,0:T(8,128)(2,1)}, bf16[512,256]{1,0:T(8,128)(2,1)S(1)}, u32[]{:S(2)}, u32[]{:S(2)}) %collective-permute-start.34) | collective-permute-done | bytes 262176 | tf_op jit(solution)/shard_map/ppermute | solution.py:45
  156.6 4.8 %collective-permute-done.35 = bf16[512,256]{1,0:T(8,128)(2,1)} collective-permute-done((bf16[512,256]{1,0:T(8,128)(2,1)S(1)}, bf16[512,256]{1,0:T(8,128)(2,1)}, u32[]{:S(2)}, u32[]{:S(2)}) %collective-permute-start.35) | collective-permute-done | bytes 262176 | tf_op jit(solution)/shard_map/ppermute | solution.py:45
  161.4 1.1 convert_add_fusion.1
  162.6 3.0 %collective-permute-start.37 = (bf16[256,256]{1,0:T(8,128)(2,1)S(1)}, bf16[256,256]{1,0:T(8,128)(2,1)S(1)}, u32[]{:S(2)}, u32[]{:S(2)}) collective-permute-start(bf16[256,256]{1,0:T(8,128)(2,1)S(1)} %select_convert_fusion), channel_id=1, source_target_pairs={{0,1},{1,0},{2,3},{3,2},{4,5},{5,4},{6,7},{7,6},{8,9},{9,8},{10,11... | collective-permute-start | bytes 393224 | tf_op jit(solution)/shard_map/ppermute | solution.py:45
  165.6 2.8 %collective-permute-start.39 = (bf16[256,256]{1,0:T(8,128)(2,1)S(1)}, bf16[256,256]{1,0:T(8,128)(2,1)S(1)}, u32[]{:S(2)}, u32[]{:S(2)}) collective-permute-start(bf16[256,256]{1,0:T(8,128)(2,1)S(1)} %get-tuple-element.44), channel_id=1, source_target_pairs={{0,4},{1,5},{2,6},{3,7},{4,0},{5,1},{6,2},{7,3},{8,12},{9,13},{10,... | collective-permute-start | bytes 393224 | tf_op jit(solution)/shard_map/ppermute | solution.py:45
  168.4 3.2 %collective-permute-start.41 = (bf16[256,256]{1,0:T(8,128)(2,1)S(1)}, bf16[256,256]{1,0:T(8,128)(2,1)S(1)}, u32[]{:S(2)}, u32[]{:S(2)}) collective-permute-start(bf16[256,256]{1,0:T(8,128)(2,1)S(1)} %get-tuple-element.46), channel_id=1, source_target_pairs={{0,6},{1,7},{2,0},{3,1},{4,2},{5,3},{6,4},{7,5},{8,14},{9,15},{10,... | collective-permute-start | bytes 393224 | tf_op jit(solution)/shard_map/ppermute | solution.py:45
  171.6 1.2 collective-permute-done.39
  172.8 2.3 %collective-permute-done.40 = bf16[256,256]{1,0:T(8,128)(2,1)S(1)} collective-permute-done((bf16[256,256]{1,0:T(8,128)(2,1)S(1)}, bf16[256,256]{1,0:T(8,128)(2,1)S(1)}, u32[]{:S(2)}, u32[]{:S(2)}) %collective-permute-start.40) | collective-permute-done | bytes 131104 | tf_op jit(solution)/shard_map/ppermute | solution.py:45
  (89 shorter events, 17.2 us)
Async XLA Ops:
  18.6 5.7 %collective-permute-start.7 = (bf16[192,512]{1,0:T(8,128)(2,1)S(1)}, bf16[192,512]{1,0:T(8,128)(2,1)S(1)}, u32[]{:S(2)}, u32[]{:S(2)}) collective-permute-start(bf16[192,512]{1,0:T(8,128)(2,1)S(1)} %bitcast.53), channel_id=1, source_target_pairs={{0,64},{8,72},{16,80},{24,88},{32,96},{40,104},{48,112},{56,120},{... | collective-permute-start | bytes 589832 | tf_op jit(solution)/shard_map/ppermute | solution.py:41
  24.3 13.4 %collective-permute-start.8 = (bf16[2,192,512]{2,1,0:T(8,128)(2,1)S(1)}, bf16[2,192,512]{2,1,0:T(8,128)(2,1)S(1)}, u32[]{:S(2)}, u32[]{:S(2)}) collective-permute-start(bf16[2,192,512]{2,1,0:T(8,128)(2,1)S(1)} %pad_maximum_fusion.refs_0_), channel_id=1, source_target_pairs={{0,16},{8,24},{16,32},{24,40},{32,48},{40,56},{48,0},{56,8},{64,80... | collective-permute-start | bytes 1179656 | tf_op jit(solution)/shard_map/ppermute | solution.py:41
  25.9 11.8 %collective-permute-start.9 = (bf16[2,192,512]{2,1,0:T(8,128)(2,1)S(1)}, bf16[2,192,512]{2,1,0:T(8,128)(2,1)S(1)}, u32[]{:S(2)}, u32[]{:S(2)}) collective-permute-start(bf16[2,192,512]{2,1,0:T(8,128)(2,1)S(1)} %pad_maximum_fusion.refs_0_), channel_id=1, source_target_pairs={{0,48},{8,56},{16,0},{24,8},{32,16},{40,24},{48,32},{56,40},{64,11... | collective-permute-start | bytes 1179656 | tf_op jit(solution)/shard_map/ppermute | solution.py:41
  27.6 7.4 %collective-permute-start.2 = (bf16[192,512]{1,0:T(8,128)(2,1)}, bf16[192,512]{1,0:T(8,128)(2,1)S(1)}, u32[]{:S(2)}, u32[]{:S(2)}) collective-permute-start(bf16[192,512]{1,0:T(8,128)(2,1)} %pick.1), channel_id=1, source_target_pairs={{0,1},{1,0},{2,3},{3,2},{4,5},{5,4},{6,7},{7,6},{8,9},{9,8},{10,11... | collective-permute-start | bytes 589832 | tf_op jit(solution)/shard_map/ppermute | solution.py:45
  28.7 7.4 %collective-permute-start = (bf16[192,512]{1,0:T(8,128)(2,1)}, bf16[192,512]{1,0:T(8,128)(2,1)}, u32[]{:S(2)}, u32[]{:S(2)}) collective-permute-start(bf16[192,512]{1,0:T(8,128)(2,1)} %pick.1), channel_id=1, source_target_pairs={{0,2},{1,3},{2,4},{3,5},{4,6},{5,7},{6,0},{7,1},{8,10},{9,11},{10,... | collective-permute-start | bytes 589832 | tf_op jit(solution)/shard_map/ppermute | solution.py:45
  29.3 9.0 %collective-permute-start.6 = (bf16[192,512]{1,0:T(8,128)(2,1)}, bf16[192,512]{1,0:T(8,128)(2,1)S(1)}, u32[]{:S(2)}, u32[]{:S(2)}) collective-permute-start(bf16[192,512]{1,0:T(8,128)(2,1)} %pick.1), channel_id=1, source_target_pairs={{0,6},{1,7},{2,0},{3,1},{4,2},{5,3},{6,4},{7,5},{8,14},{9,15},{10,... | collective-permute-start | bytes 589832 | tf_op jit(solution)/shard_map/ppermute | solution.py:45
  35.0 5.8 %collective-permute-start.3 = (bf16[192,512]{1,0:T(8,128)(2,1)S(1)}, bf16[192,512]{1,0:T(8,128)(2,1)}, u32[]{:S(2)}, u32[]{:S(2)}) collective-permute-start(bf16[192,512]{1,0:T(8,128)(2,1)S(1)} %collective-permute-done.2), channel_id=1, source_target_pairs={{0,6},{1,7},{2,0},{3,1},{4,2},{5,3},{6,4},{7,5},{8,14},{9,15},{10,... | collective-permute-start | bytes 589832 | tf_op jit(solution)/shard_map/ppermute | solution.py:45
  36.1 6.9 %collective-permute-start.5 = (bf16[192,512]{1,0:T(8,128)(2,1)S(1)}, bf16[192,512]{1,0:T(8,128)(2,1)S(1)}, u32[]{:S(2)}, u32[]{:S(2)}) collective-permute-start(bf16[192,512]{1,0:T(8,128)(2,1)S(1)} %collective-permute-done.2), channel_id=1, source_target_pairs={{0,2},{1,3},{2,4},{3,5},{4,6},{5,7},{6,0},{7,1},{8,10},{9,11},{10,... | collective-permute-start | bytes 589832 | tf_op jit(solution)/shard_map/ppermute | solution.py:45
  37.7 14.8 %collective-permute-start.15 = (bf16[2,192,512]{2,1,0:T(8,128)(2,1)S(1)}, bf16[2,192,512]{2,1,0:T(8,128)(2,1)S(1)}, u32[]{:S(2)}, u32[]{:S(2)}) collective-permute-start(bf16[2,192,512]{2,1,0:T(8,128)(2,1)S(1)} %collective-permute-done.8.a_ref.refs_0_), channel_id=1, source_target_pairs={{0,8},{8,0},{16,24},{24,16},{32,40},{40,32},{48,56},{56,48},{64,72... | collective-permute-start | bytes 1179656 | tf_op jit(solution)/shard_map/ppermute | solution.py:41
  37.7 14.8 %collective-permute-start.16 = (bf16[2,192,512]{2,1,0:T(8,128)(2,1)S(1)}, bf16[2,192,512]{2,1,0:T(8,128)(2,1)}, u32[]{:S(2)}, u32[]{:S(2)}) collective-permute-start(bf16[2,192,512]{2,1,0:T(8,128)(2,1)S(1)} %collective-permute-done.9.b_ref.refs_1_), channel_id=1, source_target_pairs={{0,8},{8,0},{16,24},{24,16},{32,40},{40,32},{48,56},{56,48},{64,72... | collective-permute-start | bytes 1179656 | tf_op jit(solution)/shard_map/ppermute | solution.py:41
  38.3 0.7 copy-start.3
  39.0 11.7 %collective-permute-start.1 = (bf16[192,512]{1,0:T(8,128)(2,1)}, bf16[192,512]{1,0:T(8,128)(2,1)}, u32[]{:S(2)}, u32[]{:S(2)}) collective-permute-start(bf16[192,512]{1,0:T(8,128)(2,1)} %collective-permute-done), channel_id=1, source_target_pairs={{0,2},{1,3},{2,4},{3,5},{4,6},{5,7},{6,0},{7,1},{8,10},{9,11},{10,... | collective-permute-start | bytes 589832 | tf_op jit(solution)/shard_map/ppermute | solution.py:45
  40.7 17.7 %collective-permute-start.18 = (bf16[2,192,512]{2,1,0:T(8,128)(2,1)S(1)}, bf16[2,192,512]{2,1,0:T(8,128)(2,1)S(1)}, u32[]{:S(2)}, u32[]{:S(2)}) collective-permute-start(bf16[2,192,512]{2,1,0:T(8,128)(2,1)S(1)} %pad_maximum_fusion.refs_0_), channel_id=1, source_target_pairs={{0,8},{8,0},{16,24},{24,16},{32,40},{40,32},{48,56},{56,48},{64,72... | collective-permute-start | bytes 1179656 | tf_op jit(solution)/shard_map/ppermute | solution.py:41
  43.6 7.0 %collective-permute-start.4 = (bf16[192,512]{1,0:T(8,128)(2,1)}, bf16[192,512]{1,0:T(8,128)(2,1)}, u32[]{:S(2)}, u32[]{:S(2)}) collective-permute-start(bf16[192,512]{1,0:T(8,128)(2,1)} %collective-permute-done.3), channel_id=1, source_target_pairs={{0,6},{1,7},{2,0},{3,1},{4,2},{5,3},{6,4},{7,5},{8,14},{9,15},{10,... | collective-permute-start | bytes 589832 | tf_op jit(solution)/shard_map/ppermute | solution.py:45
  45.2 0.9 copy-start
  46.1 0.9 copy-start.2
  47.0 0.9 copy-start.4
  47.9 0.9 copy-start.6
  58.1 25.7 %collective-permute-start.17 = (bf16[2,384,512]{2,1,0:T(8,128)(2,1)}, bf16[2,384,512]{2,1,0:T(8,128)(2,1)}, u32[]{:S(2)}, u32[]{:S(2)}) collective-permute-start(bf16[2,384,512]{2,1,0:T(8,128)(2,1)} %shard_map.73), channel_id=1, source_target_pairs={{0,8},{8,0},{16,24},{24,16},{32,40},{40,32},{48,56},{56,48},{64,72... | collective-permute-start | bytes 2359304 | tf_op jit(solution)/shard_map/ppermute | solution.py:41
  62.1 10.2 %collective-permute-start.19 = (bf16[1,384,512]{2,1,0:T(8,128)(2,1)}, bf16[1,384,512]{2,1,0:T(8,128)(2,1)}, u32[]{:S(2)}, u32[]{:S(2)}) collective-permute-start(bf16[1,384,512]{2,1,0:T(8,128)(2,1)} %shard_map.74), channel_id=1, source_target_pairs={{0,8},{8,0},{16,24},{24,16},{32,40},{40,32},{48,56},{56,48},{64,72... | collective-permute-start | bytes 1179656 | tf_op jit(solution)/shard_map/ppermute | solution.py:41
  63.2 8.6 %collective-permute-start.10 = (bf16[192,512]{1,0:T(8,128)(2,1)}, bf16[192,512]{1,0:T(8,128)(2,1)}, u32[]{:S(2)}, u32[]{:S(2)}) collective-permute-start(bf16[192,512]{1,0:T(8,128)(2,1)} %get-tuple-element.25), channel_id=1, source_target_pairs={{0,16},{8,24},{16,32},{24,40},{32,48},{40,56},{48,0},{56,8},{64,80... | collective-permute-start | bytes 589832 | tf_op jit(solution)/shard_map/ppermute | solution.py:41
  64.1 7.7 %collective-permute-start.11 = (bf16[192,512]{1,0:T(8,128)(2,1)}, bf16[192,512]{1,0:T(8,128)(2,1)}, u32[]{:S(2)}, u32[]{:S(2)}) collective-permute-start(bf16[192,512]{1,0:T(8,128)(2,1)} %get-tuple-element.26), channel_id=1, source_target_pairs={{0,48},{8,56},{16,0},{24,8},{32,16},{40,24},{48,32},{56,40},{64,11... | collective-permute-start | bytes 589832 | tf_op jit(solution)/shard_map/ppermute | solution.py:41
  71.8 7.3 %collective-permute-start.12 = (bf16[192,512]{1,0:T(8,128)(2,1)}, bf16[192,512]{1,0:T(8,128)(2,1)S(1)}, u32[]{:S(2)}, u32[]{:S(2)}) collective-permute-start(bf16[192,512]{1,0:T(8,128)(2,1)} %collective-permute-done.10.refs_0_), channel_id=1, source_target_pairs={{0,8},{8,0},{16,24},{24,16},{32,40},{40,32},{48,56},{56,48},{64,72... | collective-permute-start | bytes 589832 | tf_op jit(solution)/shard_map/ppermute | solution.py:41
  71.8 7.3 %collective-permute-start.13 = (bf16[192,512]{1,0:T(8,128)(2,1)}, bf16[192,512]{1,0:T(8,128)(2,1)S(1)}, u32[]{:S(2)}, u32[]{:S(2)}) collective-permute-start(bf16[192,512]{1,0:T(8,128)(2,1)} %collective-permute-done.11.refs_1_), channel_id=1, source_target_pairs={{0,8},{8,0},{16,24},{24,16},{32,40},{40,32},{48,56},{56,48},{64,72... | collective-permute-start | bytes 589832 | tf_op jit(solution)/shard_map/ppermute | solution.py:41
  75.7 8.1 %collective-permute-start.20 = (bf16[192,512]{1,0:T(8,128)(2,1)S(1)}, bf16[192,512]{1,0:T(8,128)(2,1)S(1)}, u32[]{:S(2)}, u32[]{:S(2)}) collective-permute-start(bf16[192,512]{1,0:T(8,128)(2,1)S(1)} %get-tuple-element.27), channel_id=1, source_target_pairs={{0,16},{8,24},{16,32},{24,40},{32,48},{40,56},{48,0},{56,8},{64,80... | collective-permute-start | bytes 589832 | tf_op jit(solution)/shard_map/ppermute | solution.py:41
  76.0 7.8 %collective-permute-start.21 = (bf16[192,512]{1,0:T(8,128)(2,1)S(1)}, bf16[192,512]{1,0:T(8,128)(2,1)S(1)}, u32[]{:S(2)}, u32[]{:S(2)}) collective-permute-start(bf16[192,512]{1,0:T(8,128)(2,1)S(1)} %get-tuple-element.28), channel_id=1, source_target_pairs={{0,48},{8,56},{16,0},{24,8},{32,16},{40,24},{48,32},{56,40},{64,11... | collective-permute-start | bytes 589832 | tf_op jit(solution)/shard_map/ppermute | solution.py:41
  82.6 13.1 %collective-permute-start.14 = (bf16[1,384,512]{2,1,0:T(8,128)(2,1)S(1)}, bf16[1,384,512]{2,1,0:T(8,128)(2,1)S(1)}, u32[]{:S(2)}, u32[]{:S(2)}) collective-permute-start(bf16[1,384,512]{2,1,0:T(8,128)(2,1)S(1)} %shard_map.72), channel_id=1, source_target_pairs={{0,8},{8,0},{16,24},{24,16},{32,40},{40,32},{48,56},{56,48},{64,72... | collective-permute-start | bytes 1179656 | tf_op jit(solution)/shard_map/ppermute | solution.py:41
  88.9 11.6 %collective-permute-start.22 = (bf16[384,512]{1,0:T(8,128)(2,1)S(1)}, bf16[384,512]{1,0:T(8,128)(2,1)S(1)}, u32[]{:S(2)}, u32[]{:S(2)}) collective-permute-start(bf16[384,512]{1,0:T(8,128)(2,1)S(1)} %get-tuple-element.29), channel_id=1, source_target_pairs={{0,16},{8,24},{16,32},{24,40},{32,48},{40,56},{48,0},{56,8},{64,80... | collective-permute-start | bytes 1179656 | tf_op jit(solution)/shard_map/ppermute | solution.py:41
  90.1 10.4 %collective-permute-start.23 = (bf16[384,512]{1,0:T(8,128)(2,1)S(1)}, bf16[384,512]{1,0:T(8,128)(2,1)S(1)}, u32[]{:S(2)}, u32[]{:S(2)}) collective-permute-start(bf16[384,512]{1,0:T(8,128)(2,1)S(1)} %get-tuple-element.30), channel_id=1, source_target_pairs={{0,48},{8,56},{16,0},{24,8},{32,16},{40,24},{48,32},{56,40},{64,11... | collective-permute-start | bytes 1179656 | tf_op jit(solution)/shard_map/ppermute | solution.py:41
  100.8 9.6 %collective-permute-start.24 = (bf16[384,512]{1,0:T(8,128)(2,1)S(1)}, bf16[384,512]{1,0:T(8,128)(2,1)S(1)}, u32[]{:S(2)}, u32[]{:S(2)}) collective-permute-start(bf16[384,512]{1,0:T(8,128)(2,1)S(1)} %fusion.2), channel_id=1, source_target_pairs={{0,64},{8,72},{16,80},{24,88},{32,96},{40,104},{48,112},{56,120},{... | collective-permute-start | bytes 1179656 | tf_op jit(solution)/shard_map/ppermute | solution.py:41
  110.5 9.9 %collective-permute-start.25 = (bf16[384,512]{1,0:T(8,128)(2,1)S(1)}, bf16[384,512]{1,0:T(8,128)(2,1)S(1)}, u32[]{:S(2)}, u32[]{:S(2)}) collective-permute-start(bf16[384,512]{1,0:T(8,128)(2,1)S(1)} %add_convert_fusion.refs_0_), channel_id=1, source_target_pairs={{0,16},{8,24},{16,32},{24,40},{32,48},{40,56},{48,0},{56,8},{64,80... | collective-permute-start | bytes 1179656 | tf_op jit(solution)/shard_map/ppermute | solution.py:41
  111.7 8.7 %collective-permute-start.26 = (bf16[384,512]{1,0:T(8,128)(2,1)S(1)}, bf16[384,512]{1,0:T(8,128)(2,1)S(1)}, u32[]{:S(2)}, u32[]{:S(2)}) collective-permute-start(bf16[384,512]{1,0:T(8,128)(2,1)S(1)} %add_convert_fusion.refs_0_), channel_id=1, source_target_pairs={{0,48},{8,56},{16,0},{24,8},{32,16},{40,24},{48,32},{56,40},{64,11... | collective-permute-start | bytes 1179656 | tf_op jit(solution)/shard_map/ppermute | solution.py:41
  113.8 10.7 %collective-permute-start.33 = (bf16[384,512]{1,0:T(8,128)(2,1)S(1)}, bf16[384,512]{1,0:T(8,128)(2,1)S(1)}, u32[]{:S(2)}, u32[]{:S(2)}) collective-permute-start(bf16[384,512]{1,0:T(8,128)(2,1)S(1)} %add_convert_fusion.refs_0_), channel_id=1, source_target_pairs={{0,8},{8,0},{16,24},{24,16},{32,40},{40,32},{48,56},{56,48},{64,72... | collective-permute-start | bytes 1179656 | tf_op jit(solution)/shard_map/ppermute | solution.py:41
  120.4 10.4 %collective-permute-start.31 = (bf16[384,512]{1,0:T(8,128)(2,1)S(1)}, bf16[384,512]{1,0:T(8,128)(2,1)S(1)}, u32[]{:S(2)}, u32[]{:S(2)}) collective-permute-start(bf16[384,512]{1,0:T(8,128)(2,1)S(1)} %collective-permute-done.25.a_ref.refs_0_), channel_id=1, source_target_pairs={{0,8},{8,0},{16,24},{24,16},{32,40},{40,32},{48,56},{56,48},{64,72... | collective-permute-start | bytes 1179656 | tf_op jit(solution)/shard_map/ppermute | solution.py:41
  120.4 10.4 %collective-permute-start.32 = (bf16[384,512]{1,0:T(8,128)(2,1)S(1)}, bf16[384,512]{1,0:T(8,128)(2,1)S(1)}, u32[]{:S(2)}, u32[]{:S(2)}) collective-permute-start(bf16[384,512]{1,0:T(8,128)(2,1)S(1)} %collective-permute-done.26.b_ref.refs_1_), channel_id=1, source_target_pairs={{0,8},{8,0},{16,24},{24,16},{32,40},{40,32},{48,56},{56,48},{64,72... | collective-permute-start | bytes 1179656 | tf_op jit(solution)/shard_map/ppermute | solution.py:41
  120.9 9.3 %collective-permute-start.27 = (bf16[192,512]{1,0:T(8,128)(2,1)S(1)}, bf16[192,512]{1,0:T(8,128)(2,1)S(1)}, u32[]{:S(2)}, u32[]{:S(2)}) collective-permute-start(bf16[192,512]{1,0:T(8,128)(2,1)S(1)} %get-tuple-element.31), channel_id=1, source_target_pairs={{0,16},{8,24},{16,32},{24,40},{32,48},{40,56},{48,0},{56,8},{64,80... | collective-permute-start | bytes 589832 | tf_op jit(solution)/shard_map/ppermute | solution.py:41
  121.1 9.2 %collective-permute-start.28 = (bf16[192,512]{1,0:T(8,128)(2,1)S(1)}, bf16[192,512]{1,0:T(8,128)(2,1)S(1)}, u32[]{:S(2)}, u32[]{:S(2)}) collective-permute-start(bf16[192,512]{1,0:T(8,128)(2,1)S(1)} %get-tuple-element.32), channel_id=1, source_target_pairs={{0,48},{8,56},{16,0},{24,8},{32,16},{40,24},{48,32},{56,40},{64,11... | collective-permute-start | bytes 589832 | tf_op jit(solution)/shard_map/ppermute | solution.py:41
  130.2 9.4 %collective-permute-start.29 = (bf16[192,512]{1,0:T(8,128)(2,1)S(1)}, bf16[192,512]{1,0:T(8,128)(2,1)S(1)}, u32[]{:S(2)}, u32[]{:S(2)}) collective-permute-start(bf16[192,512]{1,0:T(8,128)(2,1)S(1)} %collective-permute-done.27.refs_0_), channel_id=1, source_target_pairs={{0,8},{8,0},{16,24},{24,16},{32,40},{40,32},{48,56},{56,48},{64,72... | collective-permute-start | bytes 589832 | tf_op jit(solution)/shard_map/ppermute | solution.py:41
  130.3 9.3 %collective-permute-start.30 = (bf16[192,512]{1,0:T(8,128)(2,1)S(1)}, bf16[192,512]{1,0:T(8,128)(2,1)S(1)}, u32[]{:S(2)}, u32[]{:S(2)}) collective-permute-start(bf16[192,512]{1,0:T(8,128)(2,1)S(1)} %collective-permute-done.28.refs_1_), channel_id=1, source_target_pairs={{0,8},{8,0},{16,24},{24,16},{32,40},{40,32},{48,56},{56,48},{64,72... | collective-permute-start | bytes 589832 | tf_op jit(solution)/shard_map/ppermute | solution.py:41
  145.5 29.7 %copy-start.9 = (bf16[256,512]{1,0:T(8,128)(2,1)S(1)}, bf16[256,512]{1,0:T(8,128)(2,1)}, u32[]{:S(2)}) copy-start(bf16[256,512]{1,0:T(8,128)(2,1)} %orb_ref.1) | copy-start | bytes 786436
  145.6 11.0 %collective-permute-start.34 = (bf16[512,256]{1,0:T(8,128)(2,1)}, bf16[512,256]{1,0:T(8,128)(2,1)S(1)}, u32[]{:S(2)}, u32[]{:S(2)}) collective-permute-start(bf16[512,256]{1,0:T(8,128)(2,1)} %get-tuple-element.38), channel_id=1, source_target_pairs={{0,4},{1,5},{2,6},{3,7},{4,0},{5,1},{6,2},{7,3},{8,12},{9,13},{10,... | collective-permute-start | bytes 786440 | tf_op jit(solution)/shard_map/ppermute | solution.py:45
  147.4 14.0 %collective-permute-start.35 = (bf16[512,256]{1,0:T(8,128)(2,1)S(1)}, bf16[512,256]{1,0:T(8,128)(2,1)}, u32[]{:S(2)}, u32[]{:S(2)}) collective-permute-start(bf16[512,256]{1,0:T(8,128)(2,1)S(1)} %get-tuple-element.39), channel_id=1, source_target_pairs={{0,2},{1,3},{2,4},{3,5},{4,6},{5,7},{6,0},{7,1},{8,10},{9,11},{10,... | collective-permute-start | bytes 786440 | tf_op jit(solution)/shard_map/ppermute | solution.py:45
  148.2 13.2 %collective-permute-start.36 = (bf16[512,256]{1,0:T(8,128)(2,1)S(1)}, bf16[512,256]{1,0:T(8,128)(2,1)}, u32[]{:S(2)}, u32[]{:S(2)}) collective-permute-start(bf16[512,256]{1,0:T(8,128)(2,1)S(1)} %get-tuple-element.40), channel_id=1, source_target_pairs={{0,6},{1,7},{2,0},{3,1},{4,2},{5,3},{6,4},{7,5},{8,14},{9,15},{10,... | collective-permute-start | bytes 786440 | tf_op jit(solution)/shard_map/ppermute | solution.py:45
  150.6 14.9 %collective-permute-start.38 = (bf16[4,256,256]{2,1,0:T(8,128)(2,1)S(1)}, bf16[4,256,256]{2,1,0:T(8,128)(2,1)S(1)}, u32[]{:S(2)}, u32[]{:S(2)}) collective-permute-start(bf16[4,256,256]{2,1,0:T(8,128)(2,1)S(1)} %get-tuple-element.42), channel_id=1, source_target_pairs={{0,1},{1,0},{2,3},{3,2},{4,5},{5,4},{6,7},{7,6},{8,9},{9,8},{10,11... | collective-permute-start | bytes 1572872 | tf_op jit(solution)/shard_map/ppermute | solution.py:45
  162.6 9.0 %collective-permute-start.37 = (bf16[256,256]{1,0:T(8,128)(2,1)S(1)}, bf16[256,256]{1,0:T(8,128)(2,1)S(1)}, u32[]{:S(2)}, u32[]{:S(2)}) collective-permute-start(bf16[256,256]{1,0:T(8,128)(2,1)S(1)} %select_convert_fusion), channel_id=1, source_target_pairs={{0,1},{1,0},{2,3},{3,2},{4,5},{5,4},{6,7},{7,6},{8,9},{9,8},{10,11... | collective-permute-start | bytes 393224 | tf_op jit(solution)/shard_map/ppermute | solution.py:45
  165.6 7.2 %collective-permute-start.39 = (bf16[256,256]{1,0:T(8,128)(2,1)S(1)}, bf16[256,256]{1,0:T(8,128)(2,1)S(1)}, u32[]{:S(2)}, u32[]{:S(2)}) collective-permute-start(bf16[256,256]{1,0:T(8,128)(2,1)S(1)} %get-tuple-element.44), channel_id=1, source_target_pairs={{0,4},{1,5},{2,6},{3,7},{4,0},{5,1},{6,2},{7,3},{8,12},{9,13},{10,... | collective-permute-start | bytes 393224 | tf_op jit(solution)/shard_map/ppermute | solution.py:45
  168.4 6.8 %collective-permute-start.40 = (bf16[256,256]{1,0:T(8,128)(2,1)S(1)}, bf16[256,256]{1,0:T(8,128)(2,1)S(1)}, u32[]{:S(2)}, u32[]{:S(2)}) collective-permute-start(bf16[256,256]{1,0:T(8,128)(2,1)S(1)} %get-tuple-element.45), channel_id=1, source_target_pairs={{0,2},{1,3},{2,4},{3,5},{4,6},{5,7},{6,0},{7,1},{8,10},{9,11},{10,... | collective-permute-start | bytes 393224 | tf_op jit(solution)/shard_map/ppermute | solution.py:45
  168.4 6.8 %collective-permute-start.41 = (bf16[256,256]{1,0:T(8,128)(2,1)S(1)}, bf16[256,256]{1,0:T(8,128)(2,1)S(1)}, u32[]{:S(2)}, u32[]{:S(2)}) collective-permute-start(bf16[256,256]{1,0:T(8,128)(2,1)S(1)} %get-tuple-element.46), channel_id=1, source_target_pairs={{0,6},{1,7},{2,0},{3,1},{4,2},{5,3},{6,4},{7,5},{8,14},{9,15},{10,... | collective-permute-start | bytes 393224 | tf_op jit(solution)/shard_map/ppermute | solution.py:45
  (4 other events, 2.7 us)

commit v2 on v1

--- a/solution.py
+++ b/solution.py
@@ -143,9 +143,8 @@
     )(meta, piece, pot_t, *arrays, *extra)
 
 
-def exch_body(n, kind, places, meta_ref, fb_ref, *refs):
+def exch_body(n, kind, meta_ref, fb_ref, *refs):
     ts, rest = refs[:n], refs[n:]
-    k = sum(r.shape[0] for r in ts) // CH
     if kind == "first":
         out_ref, proj_ref, buf, sems, proj_sems, part, out_sems = rest
     elif kind == "next":
@@ -170,14 +169,11 @@
         return pltpu.make_async_copy(part.at[i], out_ref.at[pl.ds(i * RT, RT)], out_sems.at[i])
 
     def place(j):
-        block, at = places[j]
-        row = pl.multiple_of(meta_ref[5 + block] * CH + at, SUB)
-        return pltpu.make_async_copy(
-            ts[j], proj_ref.at[pl.ds(row, ts[j].shape[0])], proj_sems.at[j]
-        )
+        row = pl.multiple_of(meta_ref[5 + j] * CH, CH)
+        return pltpu.make_async_copy(ts[j], proj_ref.at[pl.ds(row, CH)], proj_sems.at[j])
 
     def begin(i):
-        for j in range(k):
+        for j in range(n):
             fetch(i, j).start()
         if kind != "first":
             before(i).start()
@@ -187,7 +183,7 @@
     t = jnp.concatenate([r[...] for r in ts], axis=0)
     zh = meta_ref[0]
     for i in range(4):
-        for j in range(k):
+        for j in range(n):
             fetch(i, j).wait()
         if i < 2:
             begin(i + 2)
@@ -197,9 +193,9 @@
         d = jnp.dot(buf[i], t, preferred_element_type=F32)
         if kind != "first":
             before(i).wait()
-            d = d + acc[i]
+            d = d + acc[i].astype(F32)
         if kind != "last":
-            part[i] = d
+            part[i] = d.astype(BF)
             store(i).start()
             continue
         if i < 3:
@@ -217,32 +213,28 @@
 
 
 def exch_call(kind, zh, order, cols, fb, ts, acc=None, proj=None):
-    n, k = len(ts), len(cols)
+    n = len(ts)
     vm = pl.BlockSpec(memory_space=pltpu.VMEM)
     hbm = pl.BlockSpec(memory_space=pltpu.HBM)
     shape = jax.ShapeDtypeStruct
-    tile = pltpu.VMEM((4, RT, B), F32)
+    tile = pltpu.VMEM((4, RT, B), BF)
     dma = pltpu.SemaphoreType.DMA
-    scratch = [pltpu.VMEM((4, RT, k * CH), BF), dma((4, k)), dma((n,))]
+    scratch = [pltpu.VMEM((4, RT, n * CH), BF), dma((4, n)), dma((n,))]
     if kind != "last":
         scratch += [tile, dma((4,))]
     if kind != "first":
         scratch += [tile, dma((4,))]
-    outs, out_specs = [pltpu.HBM((4 * RT, B), F32)], [hbm]
+    outs, out_specs = [pltpu.HBM((4 * RT, B), BF)], [hbm]
     if kind == "last":
         outs = [shape((RT, HB), BF)] * 3 + [
             shape((RT, HB), F32), shape((4, 256, HB), BF), shape((4, 256, HB), F32)
         ]
         out_specs = [vm] * len(outs)
     outs, out_specs = outs + [pltpu.HBM((8 * CH, B), BF)], out_specs + [hbm]
-    places, row = [], 0
-    for t in ts:
-        places.append((row // CH, row % CH))
-        row += t.shape[0]
     args = [] if acc is None else [acc, proj]
     args = [pltpu.with_memory_space_constraint(v, pltpu.HBM) for v in args]
     return pl.pallas_call(
-        functools.partial(exch_body, n, kind, places),
+        functools.partial(exch_body, n, kind),
         out_shape=outs,
         in_specs=[pl.BlockSpec(memory_space=pltpu.SMEM), hbm] + [vm] * n + [hbm] * len(args),
         out_specs=out_specs,
@@ -252,8 +244,8 @@
             vmem_limit_bytes={"first": 11, "next": 21, "last": 13}[kind] << 20
         ),
         cost_estimate=pl.CostEstimate(
-            flops=2 * 4 * RT * CH * k * B,
-            bytes_accessed=4 * RT * CH * k * 2,
+            flops=2 * 4 * RT * CH * n * B,
+            bytes_accessed=4 * RT * CH * n * 2,
             transcendentals=0,
         ),
     )(jnp.stack([zh] + order + cols).astype(jnp.int32), fb, *ts, *args)
@@ -278,9 +270,28 @@
             out_ref[q, at_ref[2 * i], at_ref[2 * i + 1]] = refs[i][q]
 
 
-def cut_body(rows_a, rows_b, a_ref, b_ref, a_out, b_out):
-    a_out[...] = a_ref[rows_a]
-    b_out[...] = b_ref[rows_b]
+def cut_body(a_ref, b_ref, a_out, b_out):
+    a_out[...] = a_ref[0]
+    b_out[...] = b_ref[1]
+
+
+def xsum_body(zh_ref, own_ref, got_2, got_1, got_3, send_ref, keep_ref):
+    total = own_ref[...]
+    for got in (got_2, got_1, got_3):
+        total = total + got[...].astype(F32)
+    lo, hi = total[:256], total[256:]
+    first = zh_ref[0] == 0
+    send_ref[...] = jnp.where(first, hi, lo).astype(BF)
+    keep_ref[...] = jnp.where(first, lo, hi)
+
+
+def last_body(orb_ref, left_ref, left_got, own_ref, got_2, got_1, got_3, out_ref):
+    left = left_ref[...] + left_got[...].astype(F32)
+    out_ref[:, :HB] = (orb_ref[:, :HB].astype(F32) - left).astype(BF)
+    right = own_ref[...]
+    for got in (got_2, got_1, got_3):
+        right = right + got[...].astype(F32)
+    out_ref[:, HB:] = (orb_ref[:, HB:].astype(F32) - right).astype(BF)
 
 
 def zsum_body(own_ref, got_ref, *outs):
@@ -331,7 +342,7 @@
     part_a = gmove(blk_a, c=1)
     part_b = gmove(blk_b, c=1)
     rows = jax.ShapeDtypeStruct((SUB, B), BF)
-    cut_a, cut_b = small_call(functools.partial(cut_body, 0, 1), [rows, rows], blk_a, blk_b)
+    cut_a, cut_b = small_call(cut_body, [rows, rows], blk_a, blk_b)
     far_0 = gmove(cut_a, y=1)
     far_1 = gmove(cut_b, y=-1)
     part_0 = gmove(far_0, c=1)
@@ -372,15 +383,10 @@
     ta = gmove(t0, y=1)
     tb = gmove(t0, y=-1)
     q0 = gmove(t0, c=1)
-    cut_a, cut_b = small_call(
-        functools.partial(cut_body, slice(0, SUB), slice(SUB, CH)), [rows, rows], ta, tb
-    )
-    t2a = gmove(cut_a, y=1)
-    t2b = gmove(cut_b, y=-1)
+    t2 = gmove(t0, y=2)
     qa = gmove(ta, c=1)
     qb = gmove(tb, c=1)
-    q2a = gmove(t2a, c=1)
-    q2b = gmove(t2b, c=1)
+    q2 = gmove(t2, c=1)
     d = 1 - c
     col = lambda core, s: core * NY + (y + s) % NY
     ident = [jnp.int32(i) for i in range(4)]
@@ -390,26 +396,25 @@
     order = [(x + s) % NX for s in (2, 1, -1, 0)]
     x_2, x_1, x_3, x_own, z_send, z_own, projection = exch_call(
         "last", zh, order, [col(c, 0), col(d, 0)], fitted_basis,
-        [t2a, t2b, q2a, q2b], acc, proj,
+        [t2, q2], acc, proj,
     )
 
-    def over_x(to_2, to_1, to_3, own):
-        total = own
-        for v, s in ((to_2, 2), (to_1, 1), (to_3, -1)):
-            total = total + pmove(v, x=s).astype(F32)
-        return total
+    def over_x(*sent):
+        return [pmove(v, x=s) for v, s in zip(sent, (2, 1, -1))]
 
     z_got = pmove(z_send, zh=1)
-    x_sum = over_x(x_2, x_1, x_3, x_own)
+    x_got = over_x(x_2, x_1, x_3)
     quarter = lambda dtype: jax.ShapeDtypeStruct((256, HB), dtype)
-    z_parts = small_call(zsum_body, [quarter(BF)] * 3 + [quarter(F32)], z_own, z_got)
-    right = over_x(*z_parts)
-    lo, hi = x_sum[:256], x_sum[256:]
-    left = jnp.where(zh == 0, lo, hi) + pmove(
-        jnp.where(zh == 0, hi, lo).astype(BF), zh=1
-    ).astype(F32)
-    exchange = jnp.concatenate([left, right], axis=1)
-    updated = (orbitals.astype(F32) - exchange).astype(BF)
+    z_2, z_1, z_3, right = small_call(zsum_body, [quarter(BF)] * 3 + [quarter(F32)], z_own, z_got)
+    right_got = over_x(z_2, z_1, z_3)
+    x_send, left = small_call(
+        xsum_body, [quarter(BF), quarter(F32)], zh.reshape(1), x_own, *x_got, smem=1
+    )
+    left_got = pmove(x_send, zh=1)
+    (updated,) = small_call(
+        last_body, [jax.ShapeDtypeStruct((256, B), BF)],
+        orbitals, left, left_got, right, *right_got,
+    )
     return (updated, projection)
 
 

time: 177 us -> 179 us (1.011)
  waiting for transfers between devices: 49.4 us -> 60.3 us
  starting transfers between devices: 48.3 us -> 42.3 us
  other arithmetic: 3.34 us -> 1.25 us
    ppermute x27 -> x25, waiting for transfers between devices: 31.2 us -> 39.1 us  [gmove(): return lax.ppermute(v, 'grid', grid_perm(**shift))]
    ppermute x27 -> x25, starting transfers between devices: 24.7 us -> 21.3 us  [gmove(): return lax.ppermute(v, 'grid', grid_perm(**shift))]
    ppermute x15, waiting for transfers between devices: 18.2 us -> 21.2 us  [pmove(): return lax.ppermute(v, 'pts', pts_perm(**shift))]
    ppermute x15, starting transfers between devices: 23.6 us -> 21 us  [pmove(): return lax.ppermute(v, 'pts', pts_perm(**shift))]
    pallas_call x3, Pallas kernels: 20.4 us -> 18 us  [exch_call(): pl.pallas_call(functools.partial(exch_body, n, kind), out_shape=outs, in_...]
    pallas_call x5 -> x6, Pallas kernels: 3.06 us -> 4 us  [small_call(): pl.pallas_call(body, out_shape=outs, in_specs=[pl.BlockSpec(memory_space=...]
  transfers between devices with their start and end apart: 42 -> 40, of which waited for: 13 -> 16; matrix products, arithmetic and copies ran while one was open for 2% -> 1% of each run, Pallas kernels for 24% -> 23%
where the time goes in v2:
time: 179 us; the launch traced here: 177 us
  waiting for transfers between devices  60.3 us (34%)
  Pallas kernels  48.7 us (27%)
  starting transfers between devices  42.3 us (24%)
  blocking collectives  15.9 us (9%)
  local copies, waits for them, and re-layouts  7.95 us (4%)
    ppermute x25, waiting for transfers between devices, gmove(): return lax.ppermute(v, 'grid', grid_perm(**shift))  39.1 us
    pallas_call x6, Pallas kernels, pair_call(): pl.pallas_call(functools.partial(pair_body, n, kind, picks), out_shape=ou...  24.7 us
    ppermute x25, starting transfers between devices, gmove(): return lax.ppermute(v, 'grid', grid_perm(**shift))  21.3 us
    ppermute x15, waiting for transfers between devices, pmove(): return lax.ppermute(v, 'pts', pts_perm(**shift))  21.2 us
    ppermute x15, starting transfers between devices, pmove(): return lax.ppermute(v, 'pts', pts_perm(**shift))  21 us
    pallas_call x3, Pallas kernels, exch_call(): pl.pallas_call(functools.partial(exch_body, n, kind), out_shape=outs, in_...  18 us
    all_to_all x1, blocking collectives, step(): slot = lax.all_to_all(picked.reshape(8, 24, B), 'pts', 0, 0, tiled=True)  15.9 us
    unnamed x20, local copies, waits for them, and re-layouts  7.01 us
  transfers between devices with their start and end apart: 40, of which 16 were waited for; matrix products, arithmetic and copies ran while one was open for 1% of the time, Pallas kernels for 23%

profile of v2, /device:TPU:0, one launch (start us, length us, event | category | flops | bytes accessed | tf_op | source)
XLA Modules:
  0.0 177.3 jit_solution(12416710719556098779)
XLA Ops:
  0.6 2.0 %pick.1 = bf16[192,512]{1,0:T(8,128)(2,1)} custom-call(s32[1,8,24]{2,1,0:T(8,128)} %rows_ref.1, s32[1,8]{1,0:T(1,128)} %count_ref.1, bf16[256,512]{1,0:T(8,128)(2,1)} %orb_ref.3), custom_call_target="tpu_custom_call" | custom-call | tf_op jit(solution)/shard_map/pick/pallas_call | solution.py:63
  2.7 15.9 %all_to_all.5 = bf16[8,24,512]{2,1,0:T(8,128)(2,1)S(1)} all-to-all(bf16[8,24,512]{2,1,0:T(8,128)(2,1)} %bitcast.42), channel_id=1, replica_groups=mesh['grid'=16,'pts'=8] {'pts'}, dimensions={0} | all-to-all | bytes 393216 | tf_op jit(solution)/shard_map/all_to_all | solution.py:335
  18.6 1.0 collective-permute-start.7
  19.6 4.7 %collective-permute-done.7 = bf16[192,512]{1,0:T(8,128)(2,1)S(1)} collective-permute-done((bf16[192,512]{1,0:T(8,128)(2,1)S(1)}, bf16[192,512]{1,0:T(8,128)(2,1)S(1)}, u32[]{:S(2)}, u32[]{:S(2)}) %collective-permute-start.7) | collective-permute-done | bytes 196640 | tf_op jit(solution)/shard_map/ppermute | solution.py:41
  24.3 1.6 collective-permute-start.8
  25.9 1.7 collective-permute-start.9
  27.6 1.1 collective-permute-start.2
  29.3 2.7 %collective-permute-start.6 = (bf16[192,512]{1,0:T(8,128)(2,1)}, bf16[192,512]{1,0:T(8,128)(2,1)S(1)}, u32[]{:S(2)}, u32[]{:S(2)}) collective-permute-start(bf16[192,512]{1,0:T(8,128)(2,1)} %pick.1), channel_id=1, source_target_pairs={{0,6},{1,7},{2,0},{3,1},{4,2},{5,3},{6,4},{7,5},{8,14},{9,15},{10,... | collective-permute-start | bytes 589832 | tf_op jit(solution)/shard_map/ppermute | solution.py:45
  32.0 3.0 %collective-permute-done.2 = bf16[192,512]{1,0:T(8,128)(2,1)S(1)} collective-permute-done((bf16[192,512]{1,0:T(8,128)(2,1)}, bf16[192,512]{1,0:T(8,128)(2,1)S(1)}, u32[]{:S(2)}, u32[]{:S(2)}) %collective-permute-start.2) | collective-permute-done | bytes 196640 | tf_op jit(solution)/shard_map/ppermute | solution.py:45
  35.0 1.1 collective-permute-start.3
  39.4 1.3 collective-permute-done.3
  40.7 2.2 %collective-permute-done.5 = bf16[192,512]{1,0:T(8,128)(2,1)S(1)} collective-permute-done((bf16[192,512]{1,0:T(8,128)(2,1)S(1)}, bf16[192,512]{1,0:T(8,128)(2,1)S(1)}, u32[]{:S(2)}, u32[]{:S(2)}) %collective-permute-start.5) | collective-permute-done | bytes 196640 | tf_op jit(solution)/shard_map/ppermute | solution.py:45
  45.1 0.9 copy-done
  46.0 0.9 copy-done.3
  49.5 1.1 shard_map.68.refs_2_
  51.2 1.1 shard_map.69
  52.3 5.7 %shard_map.73 = bf16[2,384,512]{2,1,0:T(8,128)(2,1)} custom-call(s32[4]{0:T(128)S(1)} %pad_add_fusion.6.meta_ref, bf16[1536,512]{1,0:T(8,128)(2,1)S(1)} %bitcast.36, bf16[1536,3072]{1,0:T(8,128)(2,1)} %bitcast.47, bf16[2,192,512]{2,1,0:T(8,128)(2,1)S(1)} %collective-permute-done.8.a_ref.refs_0_, ...), custom_call_target="tpu_custom_call" | custom-call | flops 2415919104 | bytes 2359296 | tf_op jit(solution)/shard_map/pallas_call | solution.py:129
  58.3 3.7 %shard_map.74 = bf16[1,384,512]{2,1,0:T(8,128)(2,1)} custom-call(s32[3]{0:T(128)S(1)} %get-tuple-element.50.meta_ref, bf16[1536,512]{1,0:T(8,128)(2,1)S(1)} %bitcast.37, bf16[1536,3072]{1,0:T(8,128)(2,1)} %bitcast.48, bf16[2,192,512]{2,1,0:T(8,128)(2,1)S(1)} %pad_maximum_fusion.refs_0_, bf16[2,192,512]{2,1,0:T(8,128)(2,1)S(1)} %collective-permute-done.18.refs_1_), custom_call_target="tpu_custom_call" | custom-call | flops 1207959552 | bytes 1179648 | tf_op jit(solution)/shard_map/pallas_call | solution.py:129
  63.9 2.4 %collective-permute-start.11 = (bf16[192,512]{1,0:T(8,128)(2,1)}, bf16[192,512]{1,0:T(8,128)(2,1)}, u32[]{:S(2)}, u32[]{:S(2)}) collective-permute-start(bf16[192,512]{1,0:T(8,128)(2,1)} %get-tuple-element.26), channel_id=1, source_target_pairs={{0,48},{8,56},{16,0},{24,8},{32,16},{40,24},{48,32},{56,40},{64,11... | collective-permute-start | bytes 589832 | tf_op jit(solution)/shard_map/ppermute | solution.py:41
  66.4 5.3 %collective-permute-done.10.refs_0_ = bf16[192,512]{1,0:T(8,128)(2,1)} collective-permute-done((bf16[192,512]{1,0:T(8,128)(2,1)}, bf16[192,512]{1,0:T(8,128)(2,1)}, u32[]{:S(2)}, u32[]{:S(2)}) %collective-permute-start.10) | collective-permute-done | bytes 196640 | tf_op jit(solution)/shard_map/ppermute | solution.py:41
  72.2 3.4 %shard_map.75 = (bf16[192,512]{1,0:T(8,128)(2,1)S(1)}, bf16[192,512]{1,0:T(8,128)(2,1)S(1)}) custom-call(s32[3]{0:T(128)S(1)} %get-tuple-element.51.meta_ref, bf16[1536,512]{1,0:T(8,128)(2,1)S(1)} %bitcast.38, bf16[1536,3072]{1,0:T(8,128)(2,1)} %bitcast.49, bf16[2,192,512]{2,1,0:T(8,128)(2,1)S(1)} %pad_maximum_fusion.refs_0_, ...), custom_call_target="tpu_custom_call" | custom-call | flops 1207959552 | bytes 1179648 | tf_op jit(solution)/shard_map/pallas_call | solution.py:129
  75.9 3.0 %collective-permute-start.21 = (bf16[192,512]{1,0:T(8,128)(2,1)S(1)}, bf16[192,512]{1,0:T(8,128)(2,1)S(1)}, u32[]{:S(2)}, u32[]{:S(2)}) collective-permute-start(bf16[192,512]{1,0:T(8,128)(2,1)S(1)} %get-tuple-element.28), channel_id=1, source_target_pairs={{0,48},{8,56},{16,0},{24,8},{32,16},{40,24},{48,32},{56,40},{64,11... | collective-permute-start | bytes 589832 | tf_op jit(solution)/shard_map/ppermute | solution.py:41
  79.0 3.4 %shard_map.72 = bf16[1,384,512]{2,1,0:T(8,128)(2,1)S(1)} custom-call(s32[3]{0:T(128)S(1)} %get-tuple-element.48.meta_ref, bf16[1536,512]{1,0:T(8,128)(2,1)S(1)} %bitcast.39, bf16[1536,3072]{1,0:T(8,128)(2,1)} %bitcast.50, bf16[192,512]{1,0:T(8,128)(2,1)} %collective-permute-done.10.refs_0_, bf16[192,512]{1,0:T(8,128)(2,1)} %collective-permute-done.11.refs_1_, ...), custom_call_target="tpu_custom_call" | custom-call | flops 1207959552 | bytes 1179648 | tf_op jit(solution)/shard_map/pallas_call | solution.py:129
  82.5 1.2 collective-permute-done.20.refs_5_
  83.7 5.1 %shard_map.76 = (bf16[384,512]{1,0:T(8,128)(2,1)S(1)}, bf16[384,512]{1,0:T(8,128)(2,1)S(1)}) custom-call(s32[4]{0:T(128)S(1)} %pad_add_fusion.4.meta_ref, bf16[1536,512]{1,0:T(8,128)(2,1)S(1)} %bitcast.40, bf16[1536,3072]{1,0:T(8,128)(2,1)} %bitcast.51, bf16[2,192,512]{2,1,0:T(8,128)(2,1)S(1)} %collective-permute-done.8.a_ref.refs_0_, ...), custom_call_target="tpu_custom_call" | custom-call | flops 2415919104 | bytes 2359296 | tf_op jit(solution)/shard_map/pallas_call | solution.py:129
  88.8 1.2 collective-permute-start.22
  90.0 2.1 %collective-permute-start.23 = (bf16[384,512]{1,0:T(8,128)(2,1)S(1)}, bf16[384,512]{1,0:T(8,128)(2,1)S(1)}, u32[]{:S(2)}, u32[]{:S(2)}) collective-permute-start(bf16[384,512]{1,0:T(8,128)(2,1)S(1)} %get-tuple-element.30), channel_id=1, source_target_pairs={{0,48},{8,56},{16,0},{24,8},{32,16},{40,24},{48,32},{56,40},{64,11... | collective-permute-start | bytes 1179656 | tf_op jit(solution)/shard_map/ppermute | solution.py:41
  92.1 3.4 %shard_map.71 = f32[384,512]{1,0:T(8,128)S(1)} custom-call(s32[3]{0:T(128)S(1)} %get-tuple-element.52.meta_ref, bf16[1536,512]{1,0:T(8,128)(2,1)S(1)} %bitcast.41, bf16[1536,3072]{1,0:T(8,128)(2,1)} %bitcast.52, bf16[192,512]{1,0:T(8,128)(2,1)} %collective-permute-done.10.refs_0_, bf16[192,512]{1,0:T(8,128)(2,1)} %collective-permute-done.11.refs_1_, ...), custom_call_target="tpu_custom_call" | custom-call | flops 1207959552 | bytes 1179648 | tf_op jit(solution)/shard_map/pallas_call | solution.py:129
  95.5 4.9 %collective-permute-done.22 = bf16[384,512]{1,0:T(8,128)(2,1)S(1)} collective-permute-done((bf16[384,512]{1,0:T(8,128)(2,1)S(1)}, bf16[384,512]{1,0:T(8,128)(2,1)S(1)}, u32[]{:S(2)}, u32[]{:S(2)}) %collective-permute-start.22) | collective-permute-done | bytes 393248 | tf_op jit(solution)/shard_map/ppermute | solution.py:41
  100.7 1.1 collective-permute-start.24
  101.7 8.5 %collective-permute-done.24 = bf16[384,512]{1,0:T(8,128)(2,1)S(1)} collective-permute-done((bf16[384,512]{1,0:T(8,128)(2,1)S(1)}, bf16[384,512]{1,0:T(8,128)(2,1)S(1)}, u32[]{:S(2)}, u32[]{:S(2)}) %collective-permute-start.24) | collective-permute-done | bytes 393248 | tf_op jit(solution)/shard_map/ppermute | solution.py:41
  110.3 1.2 collective-permute-start.27
  111.6 2.1 %collective-permute-start.28 = (bf16[384,512]{1,0:T(8,128)(2,1)S(1)}, bf16[384,512]{1,0:T(8,128)(2,1)S(1)}, u32[]{:S(2)}, u32[]{:S(2)}) collective-permute-start(bf16[384,512]{1,0:T(8,128)(2,1)S(1)} %add_convert_fusion.refs_0_), channel_id=1, source_target_pairs={{0,48},{8,56},{16,0},{24,8},{32,16},{40,24},{48,32},{56,40},{64,11... | collective-permute-start | bytes 1179656 | tf_op jit(solution)/shard_map/ppermute | solution.py:41
  114.6 8.7 %collective-permute-done.27.refs_0_ = bf16[384,512]{1,0:T(8,128)(2,1)S(1)} collective-permute-done((bf16[384,512]{1,0:T(8,128)(2,1)S(1)}, bf16[384,512]{1,0:T(8,128)(2,1)S(1)}, u32[]{:S(2)}, u32[]{:S(2)}) %collective-permute-start.27) | collective-permute-done | bytes 393248 | tf_op jit(solution)/shard_map/ppermute | solution.py:41
  123.3 4.7 %collective-permute-done.28.refs_1_ = bf16[384,512]{1,0:T(8,128)(2,1)S(1)} collective-permute-done((bf16[384,512]{1,0:T(8,128)(2,1)S(1)}, bf16[384,512]{1,0:T(8,128)(2,1)S(1)}, u32[]{:S(2)}, u32[]{:S(2)}) %collective-permute-start.28) | collective-permute-done | bytes 393248 | tf_op jit(solution)/shard_map/ppermute | solution.py:41
  128.3 1.1 collective-permute-done.25.refs_0_
  129.3 5.5 %shard_map.77 = (bf16[2048,512]{1,0:T(8,128)(2,1)}, bf16[3072,512]{1,0:T(8,128)(2,1)}) custom-call(s32[7]{0:T(128)S(1)} %stack.157.meta_ref, bf16[2048,3072]{1,0:T(8,128)(2,1)} %fb_ref.5, bf16[384,512]{1,0:T(8,128)(2,1)S(1)} %add_convert_fusion.refs_0_, bf16[384,512]{1,0:T(8,128)(2,1)S(1)} %collective-permute-done.31.refs_1_), custom_call_target="tpu_custom_call" | custom-call | flops 1610612736 | bytes 3145728 | tf_op jit(solution)/shard_map/pallas_call | solution.py:236
  134.9 7.7 %shard_map.78 = (bf16[2048,512]{1,0:T(8,128)(2,1)}, bf16[3072,512]{1,0:T(8,128)(2,1)}) custom-call(s32[9]{0:T(128)S(1)} %stack.156.meta_ref, bf16[2048,3072]{1,0:T(8,128)(2,1)} %fb_ref.5, bf16[384,512]{1,0:T(8,128)(2,1)S(1)} %collective-permute-done.27.refs_0_, ...), custom_call_target="tpu_custom_call", output_to_operand_aliasing={{1}: (7, {})} | custom-call | flops 3221225472 | bytes 6291456 | tf_op jit(solution)/shard_map/pallas_call | solution.py:236
  142.6 4.8 %shard_map.79 = (bf16[512,256]{1,0:T(8,128)(2,1)S(1)}, bf16[512,256]{1,0:T(8,128)(2,1)S(1)}, bf16[512,256]{1,0:T(8,128)(2,1)S(1)}, f32[512,256]{1,0:T(8,128)S(1)...) custom-call(s32[7]{0:T(128)S(1)} %stack.133.meta_ref, ...), custom_call_target="tpu_custom_call", output_to_operand_aliasing={{6}: (5, {})} | custom-call | flops 1610612736 | bytes 3145728 | tf_op jit(solution)/shard_map/pallas_call | solution.py:236
  147.4 3.0 %collective-permute-start.36 = (bf16[4,256,256]{2,1,0:T(8,128)(2,1)S(1)}, bf16[4,256,256]{2,1,0:T(8,128)(2,1)S(1)}, u32[]{:S(2)}, u32[]{:S(2)}) collective-permute-start(bf16[4,256,256]{2,1,0:T(8,128)(2,1)S(1)} %get-tuple-element.42), channel_id=1, source_target_pairs={{0,1},{1,0},{2,3},{3,2},{4,5},{5,4},{6,7},{7,6},{8,9},{9,8},{10,11... | collective-permute-start | bytes 1572872 | tf_op jit(solution)/shard_map/ppermute | solution.py:45
  150.7 1.7 collective-permute-start.33
  152.4 2.7 %collective-permute-start.34 = (bf16[512,256]{1,0:T(8,128)(2,1)S(1)}, bf16[512,256]{1,0:T(8,128)(2,1)S(1)}, u32[]{:S(2)}, u32[]{:S(2)}) collective-permute-start(bf16[512,256]{1,0:T(8,128)(2,1)S(1)} %get-tuple-element.38), channel_id=1, source_target_pairs={{0,6},{1,7},{2,0},{3,1},{4,2},{5,3},{6,4},{7,5},{8,14},{9,15},{10,... | collective-permute-start | bytes 786440 | tf_op jit(solution)/shard_map/ppermute | solution.py:45
  155.1 6.0 %collective-permute-done.32.got_2 = bf16[512,256]{1,0:T(8,128)(2,1)S(1)} collective-permute-done((bf16[512,256]{1,0:T(8,128)(2,1)S(1)}, bf16[512,256]{1,0:T(8,128)(2,1)S(1)}, u32[]{:S(2)}, u32[]{:S(2)}) %collective-permute-start.32) | collective-permute-done | bytes 262176 | tf_op jit(solution)/shard_map/ppermute | solution.py:45
  161.1 4.8 %collective-permute-done.33.got_1 = bf16[512,256]{1,0:T(8,128)(2,1)S(1)} collective-permute-done((bf16[512,256]{1,0:T(8,128)(2,1)S(1)}, bf16[512,256]{1,0:T(8,128)(2,1)S(1)}, u32[]{:S(2)}, u32[]{:S(2)}) %collective-permute-start.33) | collective-permute-done | bytes 262176 | tf_op jit(solution)/shard_map/ppermute | solution.py:45
  166.9 2.5 %collective-permute-start.37 = (bf16[256,256]{1,0:T(8,128)(2,1)S(1)}, bf16[256,256]{1,0:T(8,128)(2,1)S(1)}, u32[]{:S(2)}, u32[]{:S(2)}) collective-permute-start(bf16[256,256]{1,0:T(8,128)(2,1)S(1)} %get-tuple-element.44), channel_id=1, source_target_pairs={{0,4},{1,5},{2,6},{3,7},{4,0},{5,1},{6,2},{7,3},{8,12},{9,13},{10,... | collective-permute-start | bytes 393224 | tf_op jit(solution)/shard_map/ppermute | solution.py:45
  169.6 3.0 %collective-permute-start.39 = (bf16[256,256]{1,0:T(8,128)(2,1)S(1)}, bf16[256,256]{1,0:T(8,128)(2,1)S(1)}, u32[]{:S(2)}, u32[]{:S(2)}) collective-permute-start(bf16[256,256]{1,0:T(8,128)(2,1)S(1)} %get-tuple-element.46), channel_id=1, source_target_pairs={{0,6},{1,7},{2,0},{3,1},{4,2},{5,3},{6,4},{7,5},{8,14},{9,15},{10,... | collective-permute-start | bytes 393224 | tf_op jit(solution)/shard_map/ppermute | solution.py:45
  173.1 1.3 collective-permute-done.37.got_2
  174.4 2.1 %collective-permute-done.38.got_1 = bf16[256,256]{1,0:T(8,128)(2,1)S(1)} collective-permute-done((bf16[256,256]{1,0:T(8,128)(2,1)S(1)}, bf16[256,256]{1,0:T(8,128)(2,1)S(1)}, u32[]{:S(2)}, u32[]{:S(2)}) %collective-permute-start.38) | collective-permute-done | bytes 131104 | tf_op jit(solution)/shard_map/ppermute | solution.py:45
  (81 shorter events, 16.8 us)
Async XLA Ops:
  18.6 5.7 %collective-permute-start.7 = (bf16[192,512]{1,0:T(8,128)(2,1)S(1)}, bf16[192,512]{1,0:T(8,128)(2,1)S(1)}, u32[]{:S(2)}, u32[]{:S(2)}) collective-permute-start(bf16[192,512]{1,0:T(8,128)(2,1)S(1)} %bitcast.53), channel_id=1, source_target_pairs={{0,64},{8,72},{16,80},{24,88},{32,96},{40,104},{48,112},{56,120},{... | collective-permute-start | bytes 589832 | tf_op jit(solution)/shard_map/ppermute | solution.py:41
  24.3 13.4 %collective-permute-start.8 = (bf16[2,192,512]{2,1,0:T(8,128)(2,1)S(1)}, bf16[2,192,512]{2,1,0:T(8,128)(2,1)S(1)}, u32[]{:S(2)}, u32[]{:S(2)}) collective-permute-start(bf16[2,192,512]{2,1,0:T(8,128)(2,1)S(1)} %pad_maximum_fusion.refs_0_), channel_id=1, source_target_pairs={{0,16},{8,24},{16,32},{24,40},{32,48},{40,56},{48,0},{56,8},{64,80... | collective-permute-start | bytes 1179656 | tf_op jit(solution)/shard_map/ppermute | solution.py:41
  25.9 11.8 %collective-permute-start.9 = (bf16[2,192,512]{2,1,0:T(8,128)(2,1)S(1)}, bf16[2,192,512]{2,1,0:T(8,128)(2,1)S(1)}, u32[]{:S(2)}, u32[]{:S(2)}) collective-permute-start(bf16[2,192,512]{2,1,0:T(8,128)(2,1)S(1)} %pad_maximum_fusion.refs_0_), channel_id=1, source_target_pairs={{0,48},{8,56},{16,0},{24,8},{32,16},{40,24},{48,32},{56,40},{64,11... | collective-permute-start | bytes 1179656 | tf_op jit(solution)/shard_map/ppermute | solution.py:41
  27.6 7.4 %collective-permute-start.2 = (bf16[192,512]{1,0:T(8,128)(2,1)}, bf16[192,512]{1,0:T(8,128)(2,1)S(1)}, u32[]{:S(2)}, u32[]{:S(2)}) collective-permute-start(bf16[192,512]{1,0:T(8,128)(2,1)} %pick.1), channel_id=1, source_target_pairs={{0,1},{1,0},{2,3},{3,2},{4,5},{5,4},{6,7},{7,6},{8,9},{9,8},{10,11... | collective-permute-start | bytes 589832 | tf_op jit(solution)/shard_map/ppermute | solution.py:45
  28.7 7.4 %collective-permute-start = (bf16[192,512]{1,0:T(8,128)(2,1)}, bf16[192,512]{1,0:T(8,128)(2,1)}, u32[]{:S(2)}, u32[]{:S(2)}) collective-permute-start(bf16[192,512]{1,0:T(8,128)(2,1)} %pick.1), channel_id=1, source_target_pairs={{0,2},{1,3},{2,4},{3,5},{4,6},{5,7},{6,0},{7,1},{8,10},{9,11},{10,... | collective-permute-start | bytes 589832 | tf_op jit(solution)/shard_map/ppermute | solution.py:45
  29.3 9.0 %collective-permute-start.6 = (bf16[192,512]{1,0:T(8,128)(2,1)}, bf16[192,512]{1,0:T(8,128)(2,1)S(1)}, u32[]{:S(2)}, u32[]{:S(2)}) collective-permute-start(bf16[192,512]{1,0:T(8,128)(2,1)} %pick.1), channel_id=1, source_target_pairs={{0,6},{1,7},{2,0},{3,1},{4,2},{5,3},{6,4},{7,5},{8,14},{9,15},{10,... | collective-permute-start | bytes 589832 | tf_op jit(solution)/shard_map/ppermute | solution.py:45
  35.0 5.8 %collective-permute-start.3 = (bf16[192,512]{1,0:T(8,128)(2,1)S(1)}, bf16[192,512]{1,0:T(8,128)(2,1)}, u32[]{:S(2)}, u32[]{:S(2)}) collective-permute-start(bf16[192,512]{1,0:T(8,128)(2,1)S(1)} %collective-permute-done.2), channel_id=1, source_target_pairs={{0,6},{1,7},{2,0},{3,1},{4,2},{5,3},{6,4},{7,5},{8,14},{9,15},{10,... | collective-permute-start | bytes 589832 | tf_op jit(solution)/shard_map/ppermute | solution.py:45
  36.1 6.9 %collective-permute-start.5 = (bf16[192,512]{1,0:T(8,128)(2,1)S(1)}, bf16[192,512]{1,0:T(8,128)(2,1)S(1)}, u32[]{:S(2)}, u32[]{:S(2)}) collective-permute-start(bf16[192,512]{1,0:T(8,128)(2,1)S(1)} %collective-permute-done.2), channel_id=1, source_target_pairs={{0,2},{1,3},{2,4},{3,5},{4,6},{5,7},{6,0},{7,1},{8,10},{9,11},{10,... | collective-permute-start | bytes 589832 | tf_op jit(solution)/shard_map/ppermute | solution.py:45
  37.0 0.7 copy-start.2
  37.7 14.6 %collective-permute-start.15 = (bf16[2,192,512]{2,1,0:T(8,128)(2,1)S(1)}, bf16[2,192,512]{2,1,0:T(8,128)(2,1)S(1)}, u32[]{:S(2)}, u32[]{:S(2)}) collective-permute-start(bf16[2,192,512]{2,1,0:T(8,128)(2,1)S(1)} %collective-permute-done.8.a_ref.refs_0_), channel_id=1, source_target_pairs={{0,8},{8,0},{16,24},{24,16},{32,40},{40,32},{48,56},{56,48},{64,72... | collective-permute-start | bytes 1179656 | tf_op jit(solution)/shard_map/ppermute | solution.py:41
  37.7 14.6 %collective-permute-start.16 = (bf16[2,192,512]{2,1,0:T(8,128)(2,1)S(1)}, bf16[2,192,512]{2,1,0:T(8,128)(2,1)}, u32[]{:S(2)}, u32[]{:S(2)}) collective-permute-start(bf16[2,192,512]{2,1,0:T(8,128)(2,1)S(1)} %collective-permute-done.9.b_ref.refs_1_), channel_id=1, source_target_pairs={{0,8},{8,0},{16,24},{24,16},{32,40},{40,32},{48,56},{56,48},{64,72... | collective-permute-start | bytes 1179656 | tf_op jit(solution)/shard_map/ppermute | solution.py:41
  38.3 0.7 copy-start.4
  38.9 11.7 %collective-permute-start.1 = (bf16[192,512]{1,0:T(8,128)(2,1)}, bf16[192,512]{1,0:T(8,128)(2,1)}, u32[]{:S(2)}, u32[]{:S(2)}) collective-permute-start(bf16[192,512]{1,0:T(8,128)(2,1)} %collective-permute-done), channel_id=1, source_target_pairs={{0,2},{1,3},{2,4},{3,5},{4,6},{5,7},{6,0},{7,1},{8,10},{9,11},{10,... | collective-permute-start | bytes 589832 | tf_op jit(solution)/shard_map/ppermute | solution.py:45
  40.7 17.6 %collective-permute-start.18 = (bf16[2,192,512]{2,1,0:T(8,128)(2,1)S(1)}, bf16[2,192,512]{2,1,0:T(8,128)(2,1)S(1)}, u32[]{:S(2)}, u32[]{:S(2)}) collective-permute-start(bf16[2,192,512]{2,1,0:T(8,128)(2,1)S(1)} %pad_maximum_fusion.refs_0_), channel_id=1, source_target_pairs={{0,8},{8,0},{16,24},{24,16},{32,40},{40,32},{48,56},{56,48},{64,72... | collective-permute-start | bytes 1179656 | tf_op jit(solution)/shard_map/ppermute | solution.py:41
  43.6 7.0 %collective-permute-start.4 = (bf16[192,512]{1,0:T(8,128)(2,1)}, bf16[192,512]{1,0:T(8,128)(2,1)}, u32[]{:S(2)}, u32[]{:S(2)}) collective-permute-start(bf16[192,512]{1,0:T(8,128)(2,1)} %collective-permute-done.3), channel_id=1, source_target_pairs={{0,6},{1,7},{2,0},{3,1},{4,2},{5,3},{6,4},{7,5},{8,14},{9,15},{10,... | collective-permute-start | bytes 589832 | tf_op jit(solution)/shard_map/ppermute | solution.py:45
  45.1 0.9 copy-start
  46.0 0.9 copy-start.3
  47.0 0.9 copy-start.5
  47.9 0.9 copy-start.7
  48.8 0.7 copy-start.8
  58.0 25.7 %collective-permute-start.17 = (bf16[2,384,512]{2,1,0:T(8,128)(2,1)}, bf16[2,384,512]{2,1,0:T(8,128)(2,1)}, u32[]{:S(2)}, u32[]{:S(2)}) collective-permute-start(bf16[2,384,512]{2,1,0:T(8,128)(2,1)} %shard_map.73), channel_id=1, source_target_pairs={{0,8},{8,0},{16,24},{24,16},{32,40},{40,32},{48,56},{56,48},{64,72... | collective-permute-start | bytes 2359304 | tf_op jit(solution)/shard_map/ppermute | solution.py:41
  62.0 10.2 %collective-permute-start.19 = (bf16[1,384,512]{2,1,0:T(8,128)(2,1)}, bf16[1,384,512]{2,1,0:T(8,128)(2,1)}, u32[]{:S(2)}, u32[]{:S(2)}) collective-permute-start(bf16[1,384,512]{2,1,0:T(8,128)(2,1)} %shard_map.74), channel_id=1, source_target_pairs={{0,8},{8,0},{16,24},{24,16},{32,40},{40,32},{48,56},{56,48},{64,72... | collective-permute-start | bytes 1179656 | tf_op jit(solution)/shard_map/ppermute | solution.py:41
  63.1 8.6 %collective-permute-start.10 = (bf16[192,512]{1,0:T(8,128)(2,1)}, bf16[192,512]{1,0:T(8,128)(2,1)}, u32[]{:S(2)}, u32[]{:S(2)}) collective-permute-start(bf16[192,512]{1,0:T(8,128)(2,1)} %get-tuple-element.25), channel_id=1, source_target_pairs={{0,16},{8,24},{16,32},{24,40},{32,48},{40,56},{48,0},{56,8},{64,80... | collective-permute-start | bytes 589832 | tf_op jit(solution)/shard_map/ppermute | solution.py:41
  63.9 7.7 %collective-permute-start.11 = (bf16[192,512]{1,0:T(8,128)(2,1)}, bf16[192,512]{1,0:T(8,128)(2,1)}, u32[]{:S(2)}, u32[]{:S(2)}) collective-permute-start(bf16[192,512]{1,0:T(8,128)(2,1)} %get-tuple-element.26), channel_id=1, source_target_pairs={{0,48},{8,56},{16,0},{24,8},{32,16},{40,24},{48,32},{56,40},{64,11... | collective-permute-start | bytes 589832 | tf_op jit(solution)/shard_map/ppermute | solution.py:41
  71.7 7.3 %collective-permute-start.12 = (bf16[192,512]{1,0:T(8,128)(2,1)}, bf16[192,512]{1,0:T(8,128)(2,1)S(1)}, u32[]{:S(2)}, u32[]{:S(2)}) collective-permute-start(bf16[192,512]{1,0:T(8,128)(2,1)} %collective-permute-done.10.refs_0_), channel_id=1, source_target_pairs={{0,8},{8,0},{16,24},{24,16},{32,40},{40,32},{48,56},{56,48},{64,72... | collective-permute-start | bytes 589832 | tf_op jit(solution)/shard_map/ppermute | solution.py:41
  71.7 7.3 %collective-permute-start.13 = (bf16[192,512]{1,0:T(8,128)(2,1)}, bf16[192,512]{1,0:T(8,128)(2,1)S(1)}, u32[]{:S(2)}, u32[]{:S(2)}) collective-permute-start(bf16[192,512]{1,0:T(8,128)(2,1)} %collective-permute-done.11.refs_1_), channel_id=1, source_target_pairs={{0,8},{8,0},{16,24},{24,16},{32,40},{40,32},{48,56},{56,48},{64,72... | collective-permute-start | bytes 589832 | tf_op jit(solution)/shard_map/ppermute | solution.py:41
  75.6 8.1 %collective-permute-start.20 = (bf16[192,512]{1,0:T(8,128)(2,1)S(1)}, bf16[192,512]{1,0:T(8,128)(2,1)S(1)}, u32[]{:S(2)}, u32[]{:S(2)}) collective-permute-start(bf16[192,512]{1,0:T(8,128)(2,1)S(1)} %get-tuple-element.27), channel_id=1, source_target_pairs={{0,16},{8,24},{16,32},{24,40},{32,48},{40,56},{48,0},{56,8},{64,80... | collective-permute-start | bytes 589832 | tf_op jit(solution)/shard_map/ppermute | solution.py:41
  75.9 7.8 %collective-permute-start.21 = (bf16[192,512]{1,0:T(8,128)(2,1)S(1)}, bf16[192,512]{1,0:T(8,128)(2,1)S(1)}, u32[]{:S(2)}, u32[]{:S(2)}) collective-permute-start(bf16[192,512]{1,0:T(8,128)(2,1)S(1)} %get-tuple-element.28), channel_id=1, source_target_pairs={{0,48},{8,56},{16,0},{24,8},{32,16},{40,24},{48,32},{56,40},{64,11... | collective-permute-start | bytes 589832 | tf_op jit(solution)/shard_map/ppermute | solution.py:41
  82.5 13.1 %collective-permute-start.14 = (bf16[1,384,512]{2,1,0:T(8,128)(2,1)S(1)}, bf16[1,384,512]{2,1,0:T(8,128)(2,1)S(1)}, u32[]{:S(2)}, u32[]{:S(2)}) collective-permute-start(bf16[1,384,512]{2,1,0:T(8,128)(2,1)S(1)} %shard_map.72), channel_id=1, source_target_pairs={{0,8},{8,0},{16,24},{24,16},{32,40},{40,32},{48,56},{56,48},{64,72... | collective-permute-start | bytes 1179656 | tf_op jit(solution)/shard_map/ppermute | solution.py:41
  88.8 11.6 %collective-permute-start.22 = (bf16[384,512]{1,0:T(8,128)(2,1)S(1)}, bf16[384,512]{1,0:T(8,128)(2,1)S(1)}, u32[]{:S(2)}, u32[]{:S(2)}) collective-permute-start(bf16[384,512]{1,0:T(8,128)(2,1)S(1)} %get-tuple-element.29), channel_id=1, source_target_pairs={{0,16},{8,24},{16,32},{24,40},{32,48},{40,56},{48,0},{56,8},{64,80... | collective-permute-start | bytes 1179656 | tf_op jit(solution)/shard_map/ppermute | solution.py:41
  90.0 10.4 %collective-permute-start.23 = (bf16[384,512]{1,0:T(8,128)(2,1)S(1)}, bf16[384,512]{1,0:T(8,128)(2,1)S(1)}, u32[]{:S(2)}, u32[]{:S(2)}) collective-permute-start(bf16[384,512]{1,0:T(8,128)(2,1)S(1)} %get-tuple-element.30), channel_id=1, source_target_pairs={{0,48},{8,56},{16,0},{24,8},{32,16},{40,24},{48,32},{56,40},{64,11... | collective-permute-start | bytes 1179656 | tf_op jit(solution)/shard_map/ppermute | solution.py:41
  100.7 9.6 %collective-permute-start.24 = (bf16[384,512]{1,0:T(8,128)(2,1)S(1)}, bf16[384,512]{1,0:T(8,128)(2,1)S(1)}, u32[]{:S(2)}, u32[]{:S(2)}) collective-permute-start(bf16[384,512]{1,0:T(8,128)(2,1)S(1)} %fusion.2), channel_id=1, source_target_pairs={{0,64},{8,72},{16,80},{24,88},{32,96},{40,104},{48,112},{56,120},{... | collective-permute-start | bytes 1179656 | tf_op jit(solution)/shard_map/ppermute | solution.py:41
  110.3 12.9 %collective-permute-start.27 = (bf16[384,512]{1,0:T(8,128)(2,1)S(1)}, bf16[384,512]{1,0:T(8,128)(2,1)S(1)}, u32[]{:S(2)}, u32[]{:S(2)}) collective-permute-start(bf16[384,512]{1,0:T(8,128)(2,1)S(1)} %add_convert_fusion.refs_0_), channel_id=1, source_target_pairs={{0,16},{8,24},{16,32},{24,40},{32,48},{40,56},{48,0},{56,8},{64,80... | collective-permute-start | bytes 1179656 | tf_op jit(solution)/shard_map/ppermute | solution.py:41
  111.6 16.4 %collective-permute-start.28 = (bf16[384,512]{1,0:T(8,128)(2,1)S(1)}, bf16[384,512]{1,0:T(8,128)(2,1)S(1)}, u32[]{:S(2)}, u32[]{:S(2)}) collective-permute-start(bf16[384,512]{1,0:T(8,128)(2,1)S(1)} %add_convert_fusion.refs_0_), channel_id=1, source_target_pairs={{0,48},{8,56},{16,0},{24,8},{32,16},{40,24},{48,32},{56,40},{64,11... | collective-permute-start | bytes 1179656 | tf_op jit(solution)/shard_map/ppermute | solution.py:41
  113.7 15.7 %collective-permute-start.25 = (bf16[384,512]{1,0:T(8,128)(2,1)S(1)}, bf16[384,512]{1,0:T(8,128)(2,1)S(1)}, u32[]{:S(2)}, u32[]{:S(2)}) collective-permute-start(bf16[384,512]{1,0:T(8,128)(2,1)S(1)} %add_convert_fusion.refs_0_), channel_id=1, source_target_pairs={{0,32},{8,40},{16,48},{24,56},{32,0},{40,8},{48,16},{56,24},{64,96... | collective-permute-start | bytes 1179656 | tf_op jit(solution)/shard_map/ppermute | solution.py:41
  114.6 14.8 %collective-permute-start.31 = (bf16[384,512]{1,0:T(8,128)(2,1)S(1)}, bf16[384,512]{1,0:T(8,128)(2,1)S(1)}, u32[]{:S(2)}, u32[]{:S(2)}) collective-permute-start(bf16[384,512]{1,0:T(8,128)(2,1)S(1)} %add_convert_fusion.refs_0_), channel_id=1, source_target_pairs={{0,8},{8,0},{16,24},{24,16},{32,40},{40,32},{48,56},{56,48},{64,72... | collective-permute-start | bytes 1179656 | tf_op jit(solution)/shard_map/ppermute | solution.py:41
  123.3 11.6 %collective-permute-start.29 = (bf16[384,512]{1,0:T(8,128)(2,1)S(1)}, bf16[384,512]{1,0:T(8,128)(2,1)S(1)}, u32[]{:S(2)}, u32[]{:S(2)}) collective-permute-start(bf16[384,512]{1,0:T(8,128)(2,1)S(1)} %collective-permute-done.27.refs_0_), channel_id=1, source_target_pairs={{0,8},{8,0},{16,24},{24,16},{32,40},{40,32},{48,56},{56,48},{64,72... | collective-permute-start | bytes 1179656 | tf_op jit(solution)/shard_map/ppermute | solution.py:41
  128.0 6.9 %collective-permute-start.30 = (bf16[384,512]{1,0:T(8,128)(2,1)S(1)}, bf16[384,512]{1,0:T(8,128)(2,1)S(1)}, u32[]{:S(2)}, u32[]{:S(2)}) collective-permute-start(bf16[384,512]{1,0:T(8,128)(2,1)S(1)} %collective-permute-done.28.refs_1_), channel_id=1, source_target_pairs={{0,8},{8,0},{16,24},{24,16},{32,40},{40,32},{48,56},{56,48},{64,72... | collective-permute-start | bytes 1179656 | tf_op jit(solution)/shard_map/ppermute | solution.py:41
  129.3 13.3 %collective-permute-start.26 = (bf16[384,512]{1,0:T(8,128)(2,1)S(1)}, bf16[384,512]{1,0:T(8,128)(2,1)S(1)}, u32[]{:S(2)}, u32[]{:S(2)}) collective-permute-start(bf16[384,512]{1,0:T(8,128)(2,1)S(1)} %collective-permute-done.25.refs_0_), channel_id=1, source_target_pairs={{0,8},{8,0},{16,24},{24,16},{32,40},{40,32},{48,56},{56,48},{64,72... | collective-permute-start | bytes 1179656 | tf_op jit(solution)/shard_map/ppermute | solution.py:41
  142.6 33.9 %copy-start.1 = (bf16[256,512]{1,0:T(8,128)(2,1)S(1)}, bf16[256,512]{1,0:T(8,128)(2,1)}, u32[]{:S(2)}) copy-start(bf16[256,512]{1,0:T(8,128)(2,1)} %orb_ref.3) | copy-start | bytes 786436
  147.4 19.4 %collective-permute-start.36 = (bf16[4,256,256]{2,1,0:T(8,128)(2,1)S(1)}, bf16[4,256,256]{2,1,0:T(8,128)(2,1)S(1)}, u32[]{:S(2)}, u32[]{:S(2)}) collective-permute-start(bf16[4,256,256]{2,1,0:T(8,128)(2,1)S(1)} %get-tuple-element.42), channel_id=1, source_target_pairs={{0,1},{1,0},{2,3},{3,2},{4,5},{5,4},{6,7},{7,6},{8,9},{9,8},{10,11... | collective-permute-start | bytes 1572872 | tf_op jit(solution)/shard_map/ppermute | solution.py:45
  150.4 10.7 %collective-permute-start.32 = (bf16[512,256]{1,0:T(8,128)(2,1)S(1)}, bf16[512,256]{1,0:T(8,128)(2,1)S(1)}, u32[]{:S(2)}, u32[]{:S(2)}) collective-permute-start(bf16[512,256]{1,0:T(8,128)(2,1)S(1)} %get-tuple-element.36), channel_id=1, source_target_pairs={{0,4},{1,5},{2,6},{3,7},{4,0},{5,1},{6,2},{7,3},{8,12},{9,13},{10,... | collective-permute-start | bytes 786440 | tf_op jit(solution)/shard_map/ppermute | solution.py:45
  150.7 15.3 %collective-permute-start.33 = (bf16[512,256]{1,0:T(8,128)(2,1)S(1)}, bf16[512,256]{1,0:T(8,128)(2,1)S(1)}, u32[]{:S(2)}, u32[]{:S(2)}) collective-permute-start(bf16[512,256]{1,0:T(8,128)(2,1)S(1)} %get-tuple-element.37), channel_id=1, source_target_pairs={{0,2},{1,3},{2,4},{3,5},{4,6},{5,7},{6,0},{7,1},{8,10},{9,11},{10,... | collective-permute-start | bytes 786440 | tf_op jit(solution)/shard_map/ppermute | solution.py:45
  152.4 13.6 %collective-permute-start.34 = (bf16[512,256]{1,0:T(8,128)(2,1)S(1)}, bf16[512,256]{1,0:T(8,128)(2,1)S(1)}, u32[]{:S(2)}, u32[]{:S(2)}) collective-permute-start(bf16[512,256]{1,0:T(8,128)(2,1)S(1)} %get-tuple-element.38), channel_id=1, source_target_pairs={{0,6},{1,7},{2,0},{3,1},{4,2},{5,3},{6,4},{7,5},{8,14},{9,15},{10,... | collective-permute-start | bytes 786440 | tf_op jit(solution)/shard_map/ppermute | solution.py:45
  166.1 7.0 %collective-permute-start.35 = (bf16[256,256]{1,0:T(8,128)(2,1)S(1)}, bf16[256,256]{1,0:T(8,128)(2,1)S(1)}, u32[]{:S(2)}, u32[]{:S(2)}) collective-permute-start(bf16[256,256]{1,0:T(8,128)(2,1)S(1)} %get-tuple-element.40), channel_id=1, source_target_pairs={{0,1},{1,0},{2,3},{3,2},{4,5},{5,4},{6,7},{7,6},{8,9},{9,8},{10,11... | collective-permute-start | bytes 393224 | tf_op jit(solution)/shard_map/ppermute | solution.py:45
  166.9 7.5 %collective-permute-start.37 = (bf16[256,256]{1,0:T(8,128)(2,1)S(1)}, bf16[256,256]{1,0:T(8,128)(2,1)S(1)}, u32[]{:S(2)}, u32[]{:S(2)}) collective-permute-start(bf16[256,256]{1,0:T(8,128)(2,1)S(1)} %get-tuple-element.44), channel_id=1, source_target_pairs={{0,4},{1,5},{2,6},{3,7},{4,0},{5,1},{6,2},{7,3},{8,12},{9,13},{10,... | collective-permute-start | bytes 393224 | tf_op jit(solution)/shard_map/ppermute | solution.py:45
  169.4 7.1 %collective-permute-start.38 = (bf16[256,256]{1,0:T(8,128)(2,1)S(1)}, bf16[256,256]{1,0:T(8,128)(2,1)S(1)}, u32[]{:S(2)}, u32[]{:S(2)}) collective-permute-start(bf16[256,256]{1,0:T(8,128)(2,1)S(1)} %get-tuple-element.45), channel_id=1, source_target_pairs={{0,2},{1,3},{2,4},{3,5},{4,6},{5,7},{6,0},{7,1},{8,10},{9,11},{10,... | collective-permute-start | bytes 393224 | tf_op jit(solution)/shard_map/ppermute | solution.py:45
  169.6 6.9 %collective-permute-start.39 = (bf16[256,256]{1,0:T(8,128)(2,1)S(1)}, bf16[256,256]{1,0:T(8,128)(2,1)S(1)}, u32[]{:S(2)}, u32[]{:S(2)}) collective-permute-start(bf16[256,256]{1,0:T(8,128)(2,1)S(1)} %get-tuple-element.46), channel_id=1, source_target_pairs={{0,6},{1,7},{2,0},{3,1},{4,2},{5,3},{6,4},{7,5},{8,14},{9,15},{10,... | collective-permute-start | bytes 393224 | tf_op jit(solution)/shard_map/ppermute | solution.py:45
  (2 other events, 1.3 us)

commit v3 on v2

--- a/solution.py
+++ b/solution.py
@@ -316,19 +316,19 @@
     x2b = pmove(xb1, x=-1)
     spots = []
     for v, s, at in (
-        (picked, 0, zh), (zpart, 0, 1 - zh), (xa0, -1, zh), (xa1, -1, 1 - zh),
-        (xb0, 1, zh), (xb1, 1, 1 - zh), (x2a, 2, zh), (x2b, 2, 1 - zh),
+        (picked, 0, zh), (zpart, 0, 1 - zh), (xa0, -1, zh), (xb0, 1, zh),
+        (xa1, -1, 1 - zh), (xb1, 1, 1 - zh), (x2a, 2, zh), (x2b, 2, 1 - zh),
     ):
         spots.append((v.reshape(8, 24, B), (x + s) % NX, at))
     shape = jax.ShapeDtypeStruct((8, NX, 2, 24, B), BF)
-    for name, some in (("k_piece1", spots[:6]), ("k_piece2", spots[6:])):
+    piece = None
+    for some in (spots[:4], spots[4:6], spots[6:]):
         at = jnp.stack([i for _, a, b in some for i in (a, b)]).astype(i32)
-        args = [v for v, _, _ in some]
-        if name == "k_piece2":
-            args.append(piece)
+        args = [v for v, _, _ in some] + ([] if piece is None else [piece])
+        aliases = None if piece is None else {len(args): 0}
         (piece,) = small_call(
             functools.partial(piece_body, len(some)), [shape], at, *args,
-            smem=1, aliases={len(args): 0} if name == "k_piece2" else None,
+            smem=1, aliases=aliases,
         )
     piece = piece.reshape(COLS, B)
 
@@ -383,7 +383,7 @@
     ta = gmove(t0, y=1)
     tb = gmove(t0, y=-1)
     q0 = gmove(t0, c=1)
-    t2 = gmove(t0, y=2)
+    t2 = jnp.concatenate([gmove(ta[:SUB], y=1), gmove(tb[SUB:], y=-1)], 0)
     qa = gmove(ta, c=1)
     qb = gmove(tb, c=1)
     q2 = gmove(t2, c=1)

time: 179 us -> 180 us (level)
  waiting for transfers between devices: 60.3 us -> 56.3 us
  starting transfers between devices: 42.3 us -> 45.5 us
    ppermute x25 -> x26, waiting for transfers between devices: 39.1 us -> 35.2 us  [gmove(): return lax.ppermute(v, 'grid', grid_perm(**shift))]
    ppermute x25 -> x26, starting transfers between devices: 21.3 us -> 24.3 us  [gmove(): return lax.ppermute(v, 'grid', grid_perm(**shift))]
    pallas_call x6 -> x7, Pallas kernels: 4 us -> 4.86 us  [small_call(): pl.pallas_call(body, out_shape=outs, in_specs=[pl.BlockSpec(memory_space=...]
    unnamed x20 -> x23, local copies, waits for them, and re-layouts: 7.01 us -> 6.34 us
  transfers between devices with their start and end apart: 40 -> 41, of which waited for: 16 -> 16; matrix products, arithmetic and copies ran while one was open for 1% -> 1% of each run, Pallas kernels for 23% -> 24%
where the time goes in v3:
time: 180 us; the launch traced here: 177 us
  waiting for transfers between devices  56.3 us (31%)
  Pallas kernels  49.6 us (28%)
  starting transfers between devices  45.5 us (25%)
  blocking collectives  15.9 us (9%)
  local copies, waits for them, and re-layouts  7.31 us (4%)
  other arithmetic  1.89 us (1%)
    ppermute x26, waiting for transfers between devices, gmove(): return lax.ppermute(v, 'grid', grid_perm(**shift))  35.2 us
    pallas_call x6, Pallas kernels, pair_call(): pl.pallas_call(functools.partial(pair_body, n, kind, picks), out_shape=ou...  24.7 us
    ppermute x26, starting transfers between devices, gmove(): return lax.ppermute(v, 'grid', grid_perm(**shift))  24.3 us
    ppermute x15, starting transfers between devices, pmove(): return lax.ppermute(v, 'pts', pts_perm(**shift))  21.2 us
    ppermute x15, waiting for transfers between devices, pmove(): return lax.ppermute(v, 'pts', pts_perm(**shift))  21.2 us
    pallas_call x3, Pallas kernels, exch_call(): pl.pallas_call(functools.partial(exch_body, n, kind), out_shape=outs, in_...  18 us
    all_to_all x1, blocking collectives, step(): slot = lax.all_to_all(picked.reshape(8, 24, B), 'pts', 0, 0, tiled=True)  15.9 us
    unnamed x23, local copies, waits for them, and re-layouts  6.34 us
  transfers between devices with their start and end apart: 41, of which 16 were waited for; matrix products, arithmetic and copies ran while one was open for 1% of the time, Pallas kernels for 24%

profile of v3, /device:TPU:0, one launch (start us, length us, event | category | flops | bytes accessed | tf_op | source)
XLA Modules:
  0.0 177.5 jit_solution(15818186630769393452)
XLA Ops:
  0.6 2.0 %pick.1 = bf16[192,512]{1,0:T(8,128)(2,1)} custom-call(s32[1,8,24]{2,1,0:T(8,128)} %rows_ref.1, s32[1,8]{1,0:T(1,128)} %count_ref.1, bf16[256,512]{1,0:T(8,128)(2,1)} %orb_ref.3), custom_call_target="tpu_custom_call" | custom-call | tf_op jit(solution)/shard_map/pick/pallas_call | solution.py:63
  2.7 15.9 %all_to_all.5 = bf16[8,24,512]{2,1,0:T(8,128)(2,1)S(1)} all-to-all(bf16[8,24,512]{2,1,0:T(8,128)(2,1)} %bitcast.42), channel_id=1, replica_groups=mesh['grid'=16,'pts'=8] {'pts'}, dimensions={0} | all-to-all | bytes 393216 | tf_op jit(solution)/shard_map/all_to_all | solution.py:335
  18.6 1.0 collective-permute-start.7
  19.6 4.7 %collective-permute-done.7 = bf16[192,512]{1,0:T(8,128)(2,1)S(1)} collective-permute-done((bf16[192,512]{1,0:T(8,128)(2,1)S(1)}, bf16[192,512]{1,0:T(8,128)(2,1)S(1)}, u32[]{:S(2)}, u32[]{:S(2)}) %collective-permute-start.7) | collective-permute-done | bytes 196640 | tf_op jit(solution)/shard_map/ppermute | solution.py:41
  24.3 1.6 collective-permute-start.8
  25.9 1.7 collective-permute-start.9
  27.6 1.1 collective-permute-start.2
  29.3 2.7 %collective-permute-start.6 = (bf16[192,512]{1,0:T(8,128)(2,1)}, bf16[192,512]{1,0:T(8,128)(2,1)S(1)}, u32[]{:S(2)}, u32[]{:S(2)}) collective-permute-start(bf16[192,512]{1,0:T(8,128)(2,1)} %pick.1), channel_id=1, source_target_pairs={{0,6},{1,7},{2,0},{3,1},{4,2},{5,3},{6,4},{7,5},{8,14},{9,15},{10,... | collective-permute-start | bytes 589832 | tf_op jit(solution)/shard_map/ppermute | solution.py:45
  32.0 3.0 %collective-permute-done.2 = bf16[192,512]{1,0:T(8,128)(2,1)S(1)} collective-permute-done((bf16[192,512]{1,0:T(8,128)(2,1)}, bf16[192,512]{1,0:T(8,128)(2,1)S(1)}, u32[]{:S(2)}, u32[]{:S(2)}) %collective-permute-start.2) | collective-permute-done | bytes 196640 | tf_op jit(solution)/shard_map/ppermute | solution.py:45
  35.0 1.1 collective-permute-start.3
  39.3 1.4 collective-permute-done.3
  40.7 2.3 %collective-permute-done.5 = bf16[192,512]{1,0:T(8,128)(2,1)S(1)} collective-permute-done((bf16[192,512]{1,0:T(8,128)(2,1)S(1)}, bf16[192,512]{1,0:T(8,128)(2,1)S(1)}, u32[]{:S(2)}, u32[]{:S(2)}) %collective-permute-start.5) | collective-permute-done | bytes 196640 | tf_op jit(solution)/shard_map/ppermute | solution.py:45
  48.6 1.0 shard_map.68.refs_2_
  51.1 1.0 shard_map.69.refs_2_
  52.2 1.1 shard_map.70
  53.2 5.7 %shard_map.74 = bf16[2,384,512]{2,1,0:T(8,128)(2,1)} custom-call(s32[4]{0:T(128)S(1)} %pad_add_fusion.5.meta_ref, bf16[1536,512]{1,0:T(8,128)(2,1)S(1)} %bitcast.36, bf16[1536,3072]{1,0:T(8,128)(2,1)} %bitcast.47, bf16[2,192,512]{2,1,0:T(8,128)(2,1)S(1)} %collective-permute-done.8.a_ref.refs_0_, ...), custom_call_target="tpu_custom_call" | custom-call | flops 2415919104 | bytes 2359296 | tf_op jit(solution)/shard_map/pallas_call | solution.py:129
  59.2 3.7 %shard_map.75 = bf16[1,384,512]{2,1,0:T(8,128)(2,1)} custom-call(s32[3]{0:T(128)S(1)} %get-tuple-element.50.meta_ref, bf16[1536,512]{1,0:T(8,128)(2,1)S(1)} %bitcast.37, bf16[1536,3072]{1,0:T(8,128)(2,1)} %bitcast.48, bf16[2,192,512]{2,1,0:T(8,128)(2,1)S(1)} %pad_maximum_fusion.refs_0_, bf16[2,192,512]{2,1,0:T(8,128)(2,1)S(1)} %collective-permute-done.18.refs_1_), custom_call_target="tpu_custom_call" | custom-call | flops 1207959552 | bytes 1179648 | tf_op jit(solution)/shard_map/pallas_call | solution.py:129
  65.0 2.3 %collective-permute-start.11 = (bf16[192,512]{1,0:T(8,128)(2,1)}, bf16[192,512]{1,0:T(8,128)(2,1)}, u32[]{:S(2)}, u32[]{:S(2)}) collective-permute-start(bf16[192,512]{1,0:T(8,128)(2,1)} %get-tuple-element.26), channel_id=1, source_target_pairs={{0,48},{8,56},{16,0},{24,8},{32,16},{40,24},{48,32},{56,40},{64,11... | collective-permute-start | bytes 589832 | tf_op jit(solution)/shard_map/ppermute | solution.py:41
  67.3 5.3 %collective-permute-done.10.refs_0_ = bf16[192,512]{1,0:T(8,128)(2,1)} collective-permute-done((bf16[192,512]{1,0:T(8,128)(2,1)}, bf16[192,512]{1,0:T(8,128)(2,1)}, u32[]{:S(2)}, u32[]{:S(2)}) %collective-permute-start.10) | collective-permute-done | bytes 196640 | tf_op jit(solution)/shard_map/ppermute | solution.py:41
  73.1 3.4 %shard_map.76 = (bf16[192,512]{1,0:T(8,128)(2,1)S(1)}, bf16[192,512]{1,0:T(8,128)(2,1)S(1)}) custom-call(s32[3]{0:T(128)S(1)} %get-tuple-element.51.meta_ref, bf16[1536,512]{1,0:T(8,128)(2,1)S(1)} %bitcast.38, bf16[1536,3072]{1,0:T(8,128)(2,1)} %bitcast.49, bf16[2,192,512]{2,1,0:T(8,128)(2,1)S(1)} %pad_maximum_fusion.refs_0_, ...), custom_call_target="tpu_custom_call" | custom-call | flops 1207959552 | bytes 1179648 | tf_op jit(solution)/shard_map/pallas_call | solution.py:129
  76.9 2.9 %collective-permute-start.21 = (bf16[192,512]{1,0:T(8,128)(2,1)S(1)}, bf16[192,512]{1,0:T(8,128)(2,1)S(1)}, u32[]{:S(2)}, u32[]{:S(2)}) collective-permute-start(bf16[192,512]{1,0:T(8,128)(2,1)S(1)} %get-tuple-element.28), channel_id=1, source_target_pairs={{0,48},{8,56},{16,0},{24,8},{32,16},{40,24},{48,32},{56,40},{64,11... | collective-permute-start | bytes 589832 | tf_op jit(solution)/shard_map/ppermute | solution.py:41
  79.9 3.4 %shard_map.73 = bf16[1,384,512]{2,1,0:T(8,128)(2,1)S(1)} custom-call(s32[3]{0:T(128)S(1)} %get-tuple-element.48.meta_ref, bf16[1536,512]{1,0:T(8,128)(2,1)S(1)} %bitcast.39, bf16[1536,3072]{1,0:T(8,128)(2,1)} %bitcast.50, bf16[192,512]{1,0:T(8,128)(2,1)} %collective-permute-done.10.refs_0_, bf16[192,512]{1,0:T(8,128)(2,1)} %collective-permute-done.11.refs_1_, ...), custom_call_target="tpu_custom_call" | custom-call | flops 1207959552 | bytes 1179648 | tf_op jit(solution)/shard_map/pallas_call | solution.py:129
  83.5 1.2 collective-permute-done.20.refs_5_
  84.6 5.1 %shard_map.77 = (bf16[384,512]{1,0:T(8,128)(2,1)S(1)}, bf16[384,512]{1,0:T(8,128)(2,1)S(1)}) custom-call(s32[4]{0:T(128)S(1)} %pad_add_fusion.3.meta_ref, bf16[1536,512]{1,0:T(8,128)(2,1)S(1)} %bitcast.40, bf16[1536,3072]{1,0:T(8,128)(2,1)} %bitcast.51, bf16[2,192,512]{2,1,0:T(8,128)(2,1)S(1)} %collective-permute-done.8.a_ref.refs_0_, ...), custom_call_target="tpu_custom_call" | custom-call | flops 2415919104 | bytes 2359296 | tf_op jit(solution)/shard_map/pallas_call | solution.py:129
  89.7 1.2 collective-permute-start.22
  90.9 2.1 %collective-permute-start.23 = (bf16[384,512]{1,0:T(8,128)(2,1)S(1)}, bf16[384,512]{1,0:T(8,128)(2,1)S(1)}, u32[]{:S(2)}, u32[]{:S(2)}) collective-permute-start(bf16[384,512]{1,0:T(8,128)(2,1)S(1)} %get-tuple-element.30), channel_id=1, source_target_pairs={{0,48},{8,56},{16,0},{24,8},{32,16},{40,24},{48,32},{56,40},{64,11... | collective-permute-start | bytes 1179656 | tf_op jit(solution)/shard_map/ppermute | solution.py:41
  93.0 3.4 %shard_map.72 = f32[384,512]{1,0:T(8,128)S(1)} custom-call(s32[3]{0:T(128)S(1)} %get-tuple-element.52.meta_ref, bf16[1536,512]{1,0:T(8,128)(2,1)S(1)} %bitcast.41, bf16[1536,3072]{1,0:T(8,128)(2,1)} %bitcast.52, bf16[192,512]{1,0:T(8,128)(2,1)} %collective-permute-done.10.refs_0_, bf16[192,512]{1,0:T(8,128)(2,1)} %collective-permute-done.11.refs_1_, ...), custom_call_target="tpu_custom_call" | custom-call | flops 1207959552 | bytes 1179648 | tf_op jit(solution)/shard_map/pallas_call | solution.py:129
  96.5 4.9 %collective-permute-done.22 = bf16[384,512]{1,0:T(8,128)(2,1)S(1)} collective-permute-done((bf16[384,512]{1,0:T(8,128)(2,1)S(1)}, bf16[384,512]{1,0:T(8,128)(2,1)S(1)}, u32[]{:S(2)}, u32[]{:S(2)}) %collective-permute-start.22) | collective-permute-done | bytes 393248 | tf_op jit(solution)/shard_map/ppermute | solution.py:41
  101.6 1.1 collective-permute-start.24
  102.7 8.5 %collective-permute-done.24 = bf16[384,512]{1,0:T(8,128)(2,1)S(1)} collective-permute-done((bf16[384,512]{1,0:T(8,128)(2,1)S(1)}, bf16[384,512]{1,0:T(8,128)(2,1)S(1)}, u32[]{:S(2)}, u32[]{:S(2)}) %collective-permute-start.24) | collective-permute-done | bytes 393248 | tf_op jit(solution)/shard_map/ppermute | solution.py:41
  111.2 1.2 collective-permute-start.25
  112.5 2.1 %collective-permute-start.27 = (bf16[384,512]{1,0:T(8,128)(2,1)S(1)}, bf16[384,512]{1,0:T(8,128)(2,1)S(1)}, u32[]{:S(2)}, u32[]{:S(2)}) collective-permute-start(bf16[384,512]{1,0:T(8,128)(2,1)S(1)} %add_convert_fusion.refs_0_), channel_id=1, source_target_pairs={{0,48},{8,56},{16,0},{24,8},{32,16},{40,24},{48,32},{56,40},{64,11... | collective-permute-start | bytes 1179656 | tf_op jit(solution)/shard_map/ppermute | solution.py:41
  114.5 6.6 %collective-permute-done.25.refs_0_ = bf16[384,512]{1,0:T(8,128)(2,1)S(1)} collective-permute-done((bf16[384,512]{1,0:T(8,128)(2,1)S(1)}, bf16[384,512]{1,0:T(8,128)(2,1)S(1)}, u32[]{:S(2)}, u32[]{:S(2)}) %collective-permute-start.25) | collective-permute-done | bytes 393248 | tf_op jit(solution)/shard_map/ppermute | solution.py:41
  121.4 3.2 %collective-permute-start.28 = (bf16[192,512]{1,0:T(8,128)(2,1)S(1)}, bf16[192,512]{1,0:T(8,128)(2,1)S(1)}, u32[]{:S(2)}, u32[]{:S(2)}) collective-permute-start(bf16[192,512]{1,0:T(8,128)(2,1)S(1)} %slice.9), channel_id=1, source_target_pairs={{0,48},{8,56},{16,0},{24,8},{32,16},{40,24},{48,32},{56,40},{64,11... | collective-permute-start | bytes 589832 | tf_op jit(solution)/shard_map/ppermute | solution.py:41
  125.3 2.8 %collective-permute-done.26 = bf16[192,512]{1,0:T(8,128)(2,1)S(1)} collective-permute-done((bf16[192,512]{1,0:T(8,128)(2,1)S(1)}, bf16[192,512]{1,0:T(8,128)(2,1)S(1)}, u32[]{:S(2)}, u32[]{:S(2)}) %collective-permute-start.26) | collective-permute-done | bytes 196640 | tf_op jit(solution)/shard_map/ppermute | solution.py:41
  128.1 1.3 collective-permute-done.28
  129.5 5.5 %shard_map.78 = (bf16[2048,512]{1,0:T(8,128)(2,1)}, bf16[3072,512]{1,0:T(8,128)(2,1)}) custom-call(s32[7]{0:T(128)S(1)} %stack.161.meta_ref, bf16[2048,3072]{1,0:T(8,128)(2,1)} %fb_ref.5, bf16[384,512]{1,0:T(8,128)(2,1)S(1)} %add_convert_fusion.refs_0_, bf16[384,512]{1,0:T(8,128)(2,1)S(1)} %collective-permute-done.32.refs_1_), custom_call_target="tpu_custom_call" | custom-call | flops 1610612736 | bytes 3145728 | tf_op jit(solution)/shard_map/pallas_call | solution.py:236
  135.1 7.7 %shard_map.79 = (bf16[2048,512]{1,0:T(8,128)(2,1)}, bf16[3072,512]{1,0:T(8,128)(2,1)}) custom-call(s32[9]{0:T(128)S(1)} %stack.160.meta_ref, bf16[2048,3072]{1,0:T(8,128)(2,1)} %fb_ref.5, bf16[384,512]{1,0:T(8,128)(2,1)S(1)} %collective-permute-done.25.refs_0_, ...), custom_call_target="tpu_custom_call", output_to_operand_aliasing={{1}: (7, {})} | custom-call | flops 3221225472 | bytes 6291456 | tf_op jit(solution)/shard_map/pallas_call | solution.py:236
  142.8 4.8 %shard_map.80 = (bf16[512,256]{1,0:T(8,128)(2,1)S(1)}, bf16[512,256]{1,0:T(8,128)(2,1)S(1)}, bf16[512,256]{1,0:T(8,128)(2,1)S(1)}, f32[512,256]{1,0:T(8,128)S(1)...) custom-call(s32[7]{0:T(128)S(1)} %stack.136.meta_ref, ...), custom_call_target="tpu_custom_call", output_to_operand_aliasing={{6}: (5, {})} | custom-call | flops 1610612736 | bytes 3145728 | tf_op jit(solution)/shard_map/pallas_call | solution.py:236
  147.6 3.1 %collective-permute-start.37 = (bf16[4,256,256]{2,1,0:T(8,128)(2,1)S(1)}, bf16[4,256,256]{2,1,0:T(8,128)(2,1)S(1)}, u32[]{:S(2)}, u32[]{:S(2)}) collective-permute-start(bf16[4,256,256]{2,1,0:T(8,128)(2,1)S(1)} %get-tuple-element.42), channel_id=1, source_target_pairs={{0,1},{1,0},{2,3},{3,2},{4,5},{5,4},{6,7},{7,6},{8,9},{9,8},{10,11... | collective-permute-start | bytes 1572872 | tf_op jit(solution)/shard_map/ppermute | solution.py:45
  150.9 1.8 %collective-permute-start.34 = (bf16[512,256]{1,0:T(8,128)(2,1)S(1)}, bf16[512,256]{1,0:T(8,128)(2,1)S(1)}, u32[]{:S(2)}, u32[]{:S(2)}) collective-permute-start(bf16[512,256]{1,0:T(8,128)(2,1)S(1)} %get-tuple-element.37), channel_id=1, source_target_pairs={{0,2},{1,3},{2,4},{3,5},{4,6},{5,7},{6,0},{7,1},{8,10},{9,11},{10,... | collective-permute-start | bytes 786440 | tf_op jit(solution)/shard_map/ppermute | solution.py:45
  152.8 2.7 %collective-permute-start.35 = (bf16[512,256]{1,0:T(8,128)(2,1)S(1)}, bf16[512,256]{1,0:T(8,128)(2,1)S(1)}, u32[]{:S(2)}, u32[]{:S(2)}) collective-permute-start(bf16[512,256]{1,0:T(8,128)(2,1)S(1)} %get-tuple-element.38), channel_id=1, source_target_pairs={{0,6},{1,7},{2,0},{3,1},{4,2},{5,3},{6,4},{7,5},{8,14},{9,15},{10,... | collective-permute-start | bytes 786440 | tf_op jit(solution)/shard_map/ppermute | solution.py:45
  155.4 6.0 %collective-permute-done.33.got_2 = bf16[512,256]{1,0:T(8,128)(2,1)S(1)} collective-permute-done((bf16[512,256]{1,0:T(8,128)(2,1)S(1)}, bf16[512,256]{1,0:T(8,128)(2,1)S(1)}, u32[]{:S(2)}, u32[]{:S(2)}) %collective-permute-start.33) | collective-permute-done | bytes 262176 | tf_op jit(solution)/shard_map/ppermute | solution.py:45
  161.5 4.8 %collective-permute-done.34.got_1 = bf16[512,256]{1,0:T(8,128)(2,1)S(1)} collective-permute-done((bf16[512,256]{1,0:T(8,128)(2,1)S(1)}, bf16[512,256]{1,0:T(8,128)(2,1)S(1)}, u32[]{:S(2)}, u32[]{:S(2)}) %collective-permute-start.34) | collective-permute-done | bytes 262176 | tf_op jit(solution)/shard_map/ppermute | solution.py:45
  167.1 2.6 %collective-permute-start.38 = (bf16[256,256]{1,0:T(8,128)(2,1)S(1)}, bf16[256,256]{1,0:T(8,128)(2,1)S(1)}, u32[]{:S(2)}, u32[]{:S(2)}) collective-permute-start(bf16[256,256]{1,0:T(8,128)(2,1)S(1)} %get-tuple-element.44), channel_id=1, source_target_pairs={{0,4},{1,5},{2,6},{3,7},{4,0},{5,1},{6,2},{7,3},{8,12},{9,13},{10,... | collective-permute-start | bytes 393224 | tf_op jit(solution)/shard_map/ppermute | solution.py:45
  169.7 3.2 %collective-permute-start.40 = (bf16[256,256]{1,0:T(8,128)(2,1)S(1)}, bf16[256,256]{1,0:T(8,128)(2,1)S(1)}, u32[]{:S(2)}, u32[]{:S(2)}) collective-permute-start(bf16[256,256]{1,0:T(8,128)(2,1)S(1)} %get-tuple-element.46), channel_id=1, source_target_pairs={{0,6},{1,7},{2,0},{3,1},{4,2},{5,3},{6,4},{7,5},{8,14},{9,15},{10,... | collective-permute-start | bytes 393224 | tf_op jit(solution)/shard_map/ppermute | solution.py:45
  173.5 1.0 collective-permute-done.38.got_2
  174.4 2.2 %collective-permute-done.39.got_1 = bf16[256,256]{1,0:T(8,128)(2,1)S(1)} collective-permute-done((bf16[256,256]{1,0:T(8,128)(2,1)S(1)}, bf16[256,256]{1,0:T(8,128)(2,1)S(1)}, u32[]{:S(2)}, u32[]{:S(2)}) %collective-permute-start.39) | collective-permute-done | bytes 131104 | tf_op jit(solution)/shard_map/ppermute | solution.py:45
  (91 shorter events, 18.2 us)
Async XLA Ops:
  18.6 5.7 %collective-permute-start.7 = (bf16[192,512]{1,0:T(8,128)(2,1)S(1)}, bf16[192,512]{1,0:T(8,128)(2,1)S(1)}, u32[]{:S(2)}, u32[]{:S(2)}) collective-permute-start(bf16[192,512]{1,0:T(8,128)(2,1)S(1)} %bitcast.53), channel_id=1, source_target_pairs={{0,64},{8,72},{16,80},{24,88},{32,96},{40,104},{48,112},{56,120},{... | collective-permute-start | bytes 589832 | tf_op jit(solution)/shard_map/ppermute | solution.py:41
  24.3 12.7 %collective-permute-start.8 = (bf16[2,192,512]{2,1,0:T(8,128)(2,1)S(1)}, bf16[2,192,512]{2,1,0:T(8,128)(2,1)S(1)}, u32[]{:S(2)}, u32[]{:S(2)}) collective-permute-start(bf16[2,192,512]{2,1,0:T(8,128)(2,1)S(1)} %pad_maximum_fusion.refs_0_), channel_id=1, source_target_pairs={{0,16},{8,24},{16,32},{24,40},{32,48},{40,56},{48,0},{56,8},{64,80... | collective-permute-start | bytes 1179656 | tf_op jit(solution)/shard_map/ppermute | solution.py:41
  25.9 11.1 %collective-permute-start.9 = (bf16[2,192,512]{2,1,0:T(8,128)(2,1)S(1)}, bf16[2,192,512]{2,1,0:T(8,128)(2,1)S(1)}, u32[]{:S(2)}, u32[]{:S(2)}) collective-permute-start(bf16[2,192,512]{2,1,0:T(8,128)(2,1)S(1)} %pad_maximum_fusion.refs_0_), channel_id=1, source_target_pairs={{0,48},{8,56},{16,0},{24,8},{32,16},{40,24},{48,32},{56,40},{64,11... | collective-permute-start | bytes 1179656 | tf_op jit(solution)/shard_map/ppermute | solution.py:41
  27.6 7.4 %collective-permute-start.2 = (bf16[192,512]{1,0:T(8,128)(2,1)}, bf16[192,512]{1,0:T(8,128)(2,1)S(1)}, u32[]{:S(2)}, u32[]{:S(2)}) collective-permute-start(bf16[192,512]{1,0:T(8,128)(2,1)} %pick.1), channel_id=1, source_target_pairs={{0,1},{1,0},{2,3},{3,2},{4,5},{5,4},{6,7},{7,6},{8,9},{9,8},{10,11... | collective-permute-start | bytes 589832 | tf_op jit(solution)/shard_map/ppermute | solution.py:45
  28.7 7.4 %collective-permute-start = (bf16[192,512]{1,0:T(8,128)(2,1)}, bf16[192,512]{1,0:T(8,128)(2,1)}, u32[]{:S(2)}, u32[]{:S(2)}) collective-permute-start(bf16[192,512]{1,0:T(8,128)(2,1)} %pick.1), channel_id=1, source_target_pairs={{0,2},{1,3},{2,4},{3,5},{4,6},{5,7},{6,0},{7,1},{8,10},{9,11},{10,... | collective-permute-start | bytes 589832 | tf_op jit(solution)/shard_map/ppermute | solution.py:45
  29.3 8.9 %collective-permute-start.6 = (bf16[192,512]{1,0:T(8,128)(2,1)}, bf16[192,512]{1,0:T(8,128)(2,1)S(1)}, u32[]{:S(2)}, u32[]{:S(2)}) collective-permute-start(bf16[192,512]{1,0:T(8,128)(2,1)} %pick.1), channel_id=1, source_target_pairs={{0,6},{1,7},{2,0},{3,1},{4,2},{5,3},{6,4},{7,5},{8,14},{9,15},{10,... | collective-permute-start | bytes 589832 | tf_op jit(solution)/shard_map/ppermute | solution.py:45
  35.0 10.2 %copy-start.2 = (bf16[192,512]{1,0:T(8,128)(2,1)}, bf16[192,512]{1,0:T(8,128)(2,1)S(1)}, u32[]{:S(2)}) copy-start(bf16[192,512]{1,0:T(8,128)(2,1)S(1)} %collective-permute-done.2) | copy-start | bytes 589828
  35.0 5.8 %collective-permute-start.3 = (bf16[192,512]{1,0:T(8,128)(2,1)S(1)}, bf16[192,512]{1,0:T(8,128)(2,1)}, u32[]{:S(2)}, u32[]{:S(2)}) collective-permute-start(bf16[192,512]{1,0:T(8,128)(2,1)S(1)} %collective-permute-done.2), channel_id=1, source_target_pairs={{0,6},{1,7},{2,0},{3,1},{4,2},{5,3},{6,4},{7,5},{8,14},{9,15},{10,... | collective-permute-start | bytes 589832 | tf_op jit(solution)/shard_map/ppermute | solution.py:45
  36.1 6.9 %collective-permute-start.5 = (bf16[192,512]{1,0:T(8,128)(2,1)S(1)}, bf16[192,512]{1,0:T(8,128)(2,1)S(1)}, u32[]{:S(2)}, u32[]{:S(2)}) collective-permute-start(bf16[192,512]{1,0:T(8,128)(2,1)S(1)} %collective-permute-done.2), channel_id=1, source_target_pairs={{0,2},{1,3},{2,4},{3,5},{4,6},{5,7},{6,0},{7,1},{8,10},{9,11},{10,... | collective-permute-start | bytes 589832 | tf_op jit(solution)/shard_map/ppermute | solution.py:45
  37.0 16.2 %collective-permute-start.15 = (bf16[2,192,512]{2,1,0:T(8,128)(2,1)S(1)}, bf16[2,192,512]{2,1,0:T(8,128)(2,1)S(1)}, u32[]{:S(2)}, u32[]{:S(2)}) collective-permute-start(bf16[2,192,512]{2,1,0:T(8,128)(2,1)S(1)} %collective-permute-done.8.a_ref.refs_0_), channel_id=1, source_target_pairs={{0,8},{8,0},{16,24},{24,16},{32,40},{40,32},{48,56},{56,48},{64,72... | collective-permute-start | bytes 1179656 | tf_op jit(solution)/shard_map/ppermute | solution.py:41
  37.0 16.2 %collective-permute-start.16 = (bf16[2,192,512]{2,1,0:T(8,128)(2,1)S(1)}, bf16[2,192,512]{2,1,0:T(8,128)(2,1)}, u32[]{:S(2)}, u32[]{:S(2)}) collective-permute-start(bf16[2,192,512]{2,1,0:T(8,128)(2,1)S(1)} %collective-permute-done.9.b_ref.refs_1_), channel_id=1, source_target_pairs={{0,8},{8,0},{16,24},{24,16},{32,40},{40,32},{48,56},{56,48},{64,72... | collective-permute-start | bytes 1179656 | tf_op jit(solution)/shard_map/ppermute | solution.py:41
  38.9 13.3 %collective-permute-start.1 = (bf16[192,512]{1,0:T(8,128)(2,1)}, bf16[192,512]{1,0:T(8,128)(2,1)}, u32[]{:S(2)}, u32[]{:S(2)}) collective-permute-start(bf16[192,512]{1,0:T(8,128)(2,1)} %collective-permute-done), channel_id=1, source_target_pairs={{0,2},{1,3},{2,4},{3,5},{4,6},{5,7},{6,0},{7,1},{8,10},{9,11},{10,... | collective-permute-start | bytes 589832 | tf_op jit(solution)/shard_map/ppermute | solution.py:45
  40.7 18.5 %collective-permute-start.18 = (bf16[2,192,512]{2,1,0:T(8,128)(2,1)S(1)}, bf16[2,192,512]{2,1,0:T(8,128)(2,1)S(1)}, u32[]{:S(2)}, u32[]{:S(2)}) collective-permute-start(bf16[2,192,512]{2,1,0:T(8,128)(2,1)S(1)} %pad_maximum_fusion.refs_0_), channel_id=1, source_target_pairs={{0,8},{8,0},{16,24},{24,16},{32,40},{40,32},{48,56},{56,48},{64,72... | collective-permute-start | bytes 1179656 | tf_op jit(solution)/shard_map/ppermute | solution.py:41
  43.7 8.5 %collective-permute-start.4 = (bf16[192,512]{1,0:T(8,128)(2,1)}, bf16[192,512]{1,0:T(8,128)(2,1)}, u32[]{:S(2)}, u32[]{:S(2)}) collective-permute-start(bf16[192,512]{1,0:T(8,128)(2,1)} %collective-permute-done.3), channel_id=1, source_target_pairs={{0,6},{1,7},{2,0},{3,1},{4,2},{5,3},{6,4},{7,5},{8,14},{9,15},{10,... | collective-permute-start | bytes 589832 | tf_op jit(solution)/shard_map/ppermute | solution.py:45
  45.1 7.1 %copy-start.10 = (s32[4]{0:T(128)S(1)}, s32[4]{0:T(128)}, u32[]{:S(2)}) copy-start(s32[4]{0:T(128)} %add_add_fusion.at_ref) | copy-start | bytes 52
  45.2 0.9 copy-start
  46.1 0.9 copy-start.3
  47.0 0.9 copy-start.5
  49.6 0.9 copy-start.7
  58.9 25.7 %collective-permute-start.17 = (bf16[2,384,512]{2,1,0:T(8,128)(2,1)}, bf16[2,384,512]{2,1,0:T(8,128)(2,1)}, u32[]{:S(2)}, u32[]{:S(2)}) collective-permute-start(bf16[2,384,512]{2,1,0:T(8,128)(2,1)} %shard_map.74), channel_id=1, source_target_pairs={{0,8},{8,0},{16,24},{24,16},{32,40},{40,32},{48,56},{56,48},{64,72... | collective-permute-start | bytes 2359304 | tf_op jit(solution)/shard_map/ppermute | solution.py:41
  62.9 10.2 %collective-permute-start.19 = (bf16[1,384,512]{2,1,0:T(8,128)(2,1)}, bf16[1,384,512]{2,1,0:T(8,128)(2,1)}, u32[]{:S(2)}, u32[]{:S(2)}) collective-permute-start(bf16[1,384,512]{2,1,0:T(8,128)(2,1)} %shard_map.75), channel_id=1, source_target_pairs={{0,8},{8,0},{16,24},{24,16},{32,40},{40,32},{48,56},{56,48},{64,72... | collective-permute-start | bytes 1179656 | tf_op jit(solution)/shard_map/ppermute | solution.py:41
  64.0 8.6 %collective-permute-start.10 = (bf16[192,512]{1,0:T(8,128)(2,1)}, bf16[192,512]{1,0:T(8,128)(2,1)}, u32[]{:S(2)}, u32[]{:S(2)}) collective-permute-start(bf16[192,512]{1,0:T(8,128)(2,1)} %get-tuple-element.25), channel_id=1, source_target_pairs={{0,16},{8,24},{16,32},{24,40},{32,48},{40,56},{48,0},{56,8},{64,80... | collective-permute-start | bytes 589832 | tf_op jit(solution)/shard_map/ppermute | solution.py:41
  65.0 7.6 %collective-permute-start.11 = (bf16[192,512]{1,0:T(8,128)(2,1)}, bf16[192,512]{1,0:T(8,128)(2,1)}, u32[]{:S(2)}, u32[]{:S(2)}) collective-permute-start(bf16[192,512]{1,0:T(8,128)(2,1)} %get-tuple-element.26), channel_id=1, source_target_pairs={{0,48},{8,56},{16,0},{24,8},{32,16},{40,24},{48,32},{56,40},{64,11... | collective-permute-start | bytes 589832 | tf_op jit(solution)/shard_map/ppermute | solution.py:41
  72.6 7.3 %collective-permute-start.12 = (bf16[192,512]{1,0:T(8,128)(2,1)}, bf16[192,512]{1,0:T(8,128)(2,1)S(1)}, u32[]{:S(2)}, u32[]{:S(2)}) collective-permute-start(bf16[192,512]{1,0:T(8,128)(2,1)} %collective-permute-done.10.refs_0_), channel_id=1, source_target_pairs={{0,8},{8,0},{16,24},{24,16},{32,40},{40,32},{48,56},{56,48},{64,72... | collective-permute-start | bytes 589832 | tf_op jit(solution)/shard_map/ppermute | solution.py:41
  72.6 7.3 %collective-permute-start.13 = (bf16[192,512]{1,0:T(8,128)(2,1)}, bf16[192,512]{1,0:T(8,128)(2,1)S(1)}, u32[]{:S(2)}, u32[]{:S(2)}) collective-permute-start(bf16[192,512]{1,0:T(8,128)(2,1)} %collective-permute-done.11.refs_1_), channel_id=1, source_target_pairs={{0,8},{8,0},{16,24},{24,16},{32,40},{40,32},{48,56},{56,48},{64,72... | collective-permute-start | bytes 589832 | tf_op jit(solution)/shard_map/ppermute | solution.py:41
  76.5 8.1 %collective-permute-start.20 = (bf16[192,512]{1,0:T(8,128)(2,1)S(1)}, bf16[192,512]{1,0:T(8,128)(2,1)S(1)}, u32[]{:S(2)}, u32[]{:S(2)}) collective-permute-start(bf16[192,512]{1,0:T(8,128)(2,1)S(1)} %get-tuple-element.27), channel_id=1, source_target_pairs={{0,16},{8,24},{16,32},{24,40},{32,48},{40,56},{48,0},{56,8},{64,80... | collective-permute-start | bytes 589832 | tf_op jit(solution)/shard_map/ppermute | solution.py:41
  76.9 7.7 %collective-permute-start.21 = (bf16[192,512]{1,0:T(8,128)(2,1)S(1)}, bf16[192,512]{1,0:T(8,128)(2,1)S(1)}, u32[]{:S(2)}, u32[]{:S(2)}) collective-permute-start(bf16[192,512]{1,0:T(8,128)(2,1)S(1)} %get-tuple-element.28), channel_id=1, source_target_pairs={{0,48},{8,56},{16,0},{24,8},{32,16},{40,24},{48,32},{56,40},{64,11... | collective-permute-start | bytes 589832 | tf_op jit(solution)/shard_map/ppermute | solution.py:41
  83.4 13.1 %collective-permute-start.14 = (bf16[1,384,512]{2,1,0:T(8,128)(2,1)S(1)}, bf16[1,384,512]{2,1,0:T(8,128)(2,1)S(1)}, u32[]{:S(2)}, u32[]{:S(2)}) collective-permute-start(bf16[1,384,512]{2,1,0:T(8,128)(2,1)S(1)} %shard_map.73), channel_id=1, source_target_pairs={{0,8},{8,0},{16,24},{24,16},{32,40},{40,32},{48,56},{56,48},{64,72... | collective-permute-start | bytes 1179656 | tf_op jit(solution)/shard_map/ppermute | solution.py:41
  89.7 11.6 %collective-permute-start.22 = (bf16[384,512]{1,0:T(8,128)(2,1)S(1)}, bf16[384,512]{1,0:T(8,128)(2,1)S(1)}, u32[]{:S(2)}, u32[]{:S(2)}) collective-permute-start(bf16[384,512]{1,0:T(8,128)(2,1)S(1)} %get-tuple-element.29), channel_id=1, source_target_pairs={{0,16},{8,24},{16,32},{24,40},{32,48},{40,56},{48,0},{56,8},{64,80... | collective-permute-start | bytes 1179656 | tf_op jit(solution)/shard_map/ppermute | solution.py:41
  90.9 10.4 %collective-permute-start.23 = (bf16[384,512]{1,0:T(8,128)(2,1)S(1)}, bf16[384,512]{1,0:T(8,128)(2,1)S(1)}, u32[]{:S(2)}, u32[]{:S(2)}) collective-permute-start(bf16[384,512]{1,0:T(8,128)(2,1)S(1)} %get-tuple-element.30), channel_id=1, source_target_pairs={{0,48},{8,56},{16,0},{24,8},{32,16},{40,24},{48,32},{56,40},{64,11... | collective-permute-start | bytes 1179656 | tf_op jit(solution)/shard_map/ppermute | solution.py:41
  101.6 9.6 %collective-permute-start.24 = (bf16[384,512]{1,0:T(8,128)(2,1)S(1)}, bf16[384,512]{1,0:T(8,128)(2,1)S(1)}, u32[]{:S(2)}, u32[]{:S(2)}) collective-permute-start(bf16[384,512]{1,0:T(8,128)(2,1)S(1)} %fusion.2), channel_id=1, source_target_pairs={{0,64},{8,72},{16,80},{24,88},{32,96},{40,104},{48,112},{56,120},{... | collective-permute-start | bytes 1179656 | tf_op jit(solution)/shard_map/ppermute | solution.py:41
  111.2 9.9 %collective-permute-start.25 = (bf16[384,512]{1,0:T(8,128)(2,1)S(1)}, bf16[384,512]{1,0:T(8,128)(2,1)S(1)}, u32[]{:S(2)}, u32[]{:S(2)}) collective-permute-start(bf16[384,512]{1,0:T(8,128)(2,1)S(1)} %add_convert_fusion.refs_0_), channel_id=1, source_target_pairs={{0,16},{8,24},{16,32},{24,40},{32,48},{40,56},{48,0},{56,8},{64,80... | collective-permute-start | bytes 1179656 | tf_op jit(solution)/shard_map/ppermute | solution.py:41
  112.5 8.9 %collective-permute-start.27 = (bf16[384,512]{1,0:T(8,128)(2,1)S(1)}, bf16[384,512]{1,0:T(8,128)(2,1)S(1)}, u32[]{:S(2)}, u32[]{:S(2)}) collective-permute-start(bf16[384,512]{1,0:T(8,128)(2,1)S(1)} %add_convert_fusion.refs_0_), channel_id=1, source_target_pairs={{0,48},{8,56},{16,0},{24,8},{32,16},{40,24},{48,32},{56,40},{64,11... | collective-permute-start | bytes 1179656 | tf_op jit(solution)/shard_map/ppermute | solution.py:41
  121.2 6.9 %collective-permute-start.26 = (bf16[192,512]{1,0:T(8,128)(2,1)S(1)}, bf16[192,512]{1,0:T(8,128)(2,1)S(1)}, u32[]{:S(2)}, u32[]{:S(2)}) collective-permute-start(bf16[192,512]{1,0:T(8,128)(2,1)S(1)} %slice.8), channel_id=1, source_target_pairs={{0,16},{8,24},{16,32},{24,40},{32,48},{40,56},{48,0},{56,8},{64,80... | collective-permute-start | bytes 589832 | tf_op jit(solution)/shard_map/ppermute | solution.py:41
  121.3 8.3 %collective-permute-start.32 = (bf16[384,512]{1,0:T(8,128)(2,1)S(1)}, bf16[384,512]{1,0:T(8,128)(2,1)S(1)}, u32[]{:S(2)}, u32[]{:S(2)}) collective-permute-start(bf16[384,512]{1,0:T(8,128)(2,1)S(1)} %add_convert_fusion.refs_0_), channel_id=1, source_target_pairs={{0,8},{8,0},{16,24},{24,16},{32,40},{40,32},{48,56},{56,48},{64,72... | collective-permute-start | bytes 1179656 | tf_op jit(solution)/shard_map/ppermute | solution.py:41
  121.4 8.0 %collective-permute-start.28 = (bf16[192,512]{1,0:T(8,128)(2,1)S(1)}, bf16[192,512]{1,0:T(8,128)(2,1)S(1)}, u32[]{:S(2)}, u32[]{:S(2)}) collective-permute-start(bf16[192,512]{1,0:T(8,128)(2,1)S(1)} %slice.9), channel_id=1, source_target_pairs={{0,48},{8,56},{16,0},{24,8},{32,16},{40,24},{48,32},{56,40},{64,11... | collective-permute-start | bytes 589832 | tf_op jit(solution)/shard_map/ppermute | solution.py:41
  124.6 10.5 %collective-permute-start.30 = (bf16[384,512]{1,0:T(8,128)(2,1)S(1)}, bf16[384,512]{1,0:T(8,128)(2,1)S(1)}, u32[]{:S(2)}, u32[]{:S(2)}) collective-permute-start(bf16[384,512]{1,0:T(8,128)(2,1)S(1)} %collective-permute-done.25.refs_0_), channel_id=1, source_target_pairs={{0,8},{8,0},{16,24},{24,16},{32,40},{40,32},{48,56},{56,48},{64,72... | collective-permute-start | bytes 1179656 | tf_op jit(solution)/shard_map/ppermute | solution.py:41
  124.8 10.3 %collective-permute-start.31 = (bf16[384,512]{1,0:T(8,128)(2,1)S(1)}, bf16[384,512]{1,0:T(8,128)(2,1)S(1)}, u32[]{:S(2)}, u32[]{:S(2)}) collective-permute-start(bf16[384,512]{1,0:T(8,128)(2,1)S(1)} %collective-permute-done.27.refs_1_), channel_id=1, source_target_pairs={{0,8},{8,0},{16,24},{24,16},{32,40},{40,32},{48,56},{56,48},{64,72... | collective-permute-start | bytes 1179656 | tf_op jit(solution)/shard_map/ppermute | solution.py:41
  129.4 13.4 %collective-permute-start.29 = (bf16[384,512]{1,0:T(8,128)(2,1)S(1)}, bf16[384,512]{1,0:T(8,128)(2,1)S(1)}, u32[]{:S(2)}, u32[]{:S(2)}) collective-permute-start(bf16[384,512]{1,0:T(8,128)(2,1)S(1)} %constant_dynamic-update-slice_fusion.refs_0_), channel_id=1, source_target_pairs={{0,8},{8,0},{16,24},{24,16},{32,40},{40,32},{48,56},{56,48},{64,72... | collective-permute-start | bytes 1179656 | tf_op jit(solution)/shard_map/ppermute | solution.py:41
  142.8 33.8 %copy-start.1 = (bf16[256,512]{1,0:T(8,128)(2,1)S(1)}, bf16[256,512]{1,0:T(8,128)(2,1)}, u32[]{:S(2)}) copy-start(bf16[256,512]{1,0:T(8,128)(2,1)} %orb_ref.3) | copy-start | bytes 786436
  147.6 19.4 %collective-permute-start.37 = (bf16[4,256,256]{2,1,0:T(8,128)(2,1)S(1)}, bf16[4,256,256]{2,1,0:T(8,128)(2,1)S(1)}, u32[]{:S(2)}, u32[]{:S(2)}) collective-permute-start(bf16[4,256,256]{2,1,0:T(8,128)(2,1)S(1)} %get-tuple-element.42), channel_id=1, source_target_pairs={{0,1},{1,0},{2,3},{3,2},{4,5},{5,4},{6,7},{7,6},{8,9},{9,8},{10,11... | collective-permute-start | bytes 1572872 | tf_op jit(solution)/shard_map/ppermute | solution.py:45
  150.7 10.7 %collective-permute-start.33 = (bf16[512,256]{1,0:T(8,128)(2,1)S(1)}, bf16[512,256]{1,0:T(8,128)(2,1)S(1)}, u32[]{:S(2)}, u32[]{:S(2)}) collective-permute-start(bf16[512,256]{1,0:T(8,128)(2,1)S(1)} %get-tuple-element.36), channel_id=1, source_target_pairs={{0,4},{1,5},{2,6},{3,7},{4,0},{5,1},{6,2},{7,3},{8,12},{9,13},{10,... | collective-permute-start | bytes 786440 | tf_op jit(solution)/shard_map/ppermute | solution.py:45
  150.9 15.3 %collective-permute-start.34 = (bf16[512,256]{1,0:T(8,128)(2,1)S(1)}, bf16[512,256]{1,0:T(8,128)(2,1)S(1)}, u32[]{:S(2)}, u32[]{:S(2)}) collective-permute-start(bf16[512,256]{1,0:T(8,128)(2,1)S(1)} %get-tuple-element.37), channel_id=1, source_target_pairs={{0,2},{1,3},{2,4},{3,5},{4,6},{5,7},{6,0},{7,1},{8,10},{9,11},{10,... | collective-permute-start | bytes 786440 | tf_op jit(solution)/shard_map/ppermute | solution.py:45
  152.8 13.5 %collective-permute-start.35 = (bf16[512,256]{1,0:T(8,128)(2,1)S(1)}, bf16[512,256]{1,0:T(8,128)(2,1)S(1)}, u32[]{:S(2)}, u32[]{:S(2)}) collective-permute-start(bf16[512,256]{1,0:T(8,128)(2,1)S(1)} %get-tuple-element.38), channel_id=1, source_target_pairs={{0,6},{1,7},{2,0},{3,1},{4,2},{5,3},{6,4},{7,5},{8,14},{9,15},{10,... | collective-permute-start | bytes 786440 | tf_op jit(solution)/shard_map/ppermute | solution.py:45
  166.4 7.0 %collective-permute-start.36 = (bf16[256,256]{1,0:T(8,128)(2,1)S(1)}, bf16[256,256]{1,0:T(8,128)(2,1)S(1)}, u32[]{:S(2)}, u32[]{:S(2)}) collective-permute-start(bf16[256,256]{1,0:T(8,128)(2,1)S(1)} %get-tuple-element.40), channel_id=1, source_target_pairs={{0,1},{1,0},{2,3},{3,2},{4,5},{5,4},{6,7},{7,6},{8,9},{9,8},{10,11... | collective-permute-start | bytes 393224 | tf_op jit(solution)/shard_map/ppermute | solution.py:45
  167.1 7.3 %collective-permute-start.38 = (bf16[256,256]{1,0:T(8,128)(2,1)S(1)}, bf16[256,256]{1,0:T(8,128)(2,1)S(1)}, u32[]{:S(2)}, u32[]{:S(2)}) collective-permute-start(bf16[256,256]{1,0:T(8,128)(2,1)S(1)} %get-tuple-element.44), channel_id=1, source_target_pairs={{0,4},{1,5},{2,6},{3,7},{4,0},{5,1},{6,2},{7,3},{8,12},{9,13},{10,... | collective-permute-start | bytes 393224 | tf_op jit(solution)/shard_map/ppermute | solution.py:45
  169.7 6.9 %collective-permute-start.39 = (bf16[256,256]{1,0:T(8,128)(2,1)S(1)}, bf16[256,256]{1,0:T(8,128)(2,1)S(1)}, u32[]{:S(2)}, u32[]{:S(2)}) collective-permute-start(bf16[256,256]{1,0:T(8,128)(2,1)S(1)} %get-tuple-element.45), channel_id=1, source_target_pairs={{0,2},{1,3},{2,4},{3,5},{4,6},{5,7},{6,0},{7,1},{8,10},{9,11},{10,... | collective-permute-start | bytes 393224 | tf_op jit(solution)/shard_map/ppermute | solution.py:45
  169.7 6.9 %collective-permute-start.40 = (bf16[256,256]{1,0:T(8,128)(2,1)S(1)}, bf16[256,256]{1,0:T(8,128)(2,1)S(1)}, u32[]{:S(2)}, u32[]{:S(2)}) collective-permute-start(bf16[256,256]{1,0:T(8,128)(2,1)S(1)} %get-tuple-element.46), channel_id=1, source_target_pairs={{0,6},{1,7},{2,0},{3,1},{4,2},{5,3},{6,4},{7,5},{8,14},{9,15},{10,... | collective-permute-start | bytes 393224 | tf_op jit(solution)/shard_map/ppermute | solution.py:45
  (4 other events, 2.6 us)
